TPU v7x, 512 devices: a whole 4x8x8 slice. The times are simulated.
512 devices in a mesh: region: 8 (over z), blk: 64 (over y, x, core).
Axes of the slice: x: 4, y: 8, z: 8, core: 2. Of those that a mesh axis runs over, the one named last changes fastest.
Arguments:
- ensemble: float32 [1024, 256, 128], P(('region', 'blk'))
- observed: float32 [1024, 256, 128], P(('region', 'blk')), may hold values from -6 to 6
- obs_var: float32 [1024, 256], P(('region', 'blk')), may hold values from 0.5 to 2
- ridge: float32 [1024], P(('region', 'blk')), may hold values from 0.05 to 0.5
- pred_back: int32 [1024, 12], P(('region', 'blk')), may hold values from 0 to 16, as said below
- bounds: float32 [2], replicated, may hold values from 0.2 to 6, as said below
Outputs:
- analysis: float32 [1024, 256, 128], P(('region', 'blk'))
Inputs may be any that keep to these rules, and one draw needn't show every extreme that they name: `pred_back`: each row holds distinct distances among 1 to 16, never more than the block's own index, with 0 for an empty slot; the last block fills all 12 slots. bounds[0] < bounds[1].
All inputs are finite; a program needn't handle non-finite values.
Results may differ from a plain program's by a relative error of at most 0.0003.
Values sent between devices are 32-bit elements; how exact they have to be, the bound alone decides.
No kernel may reach another device: no remote copies, remote signals or barrier semaphores. Data moves between devices by JAX's collectives and lax.ppermute only.
A program may use at most 192 MiB of HBM per device.

v0:
```python
import jax
import jax.numpy as jnp
from jax import lax
from jax.sharding import PartitionSpec as P

REACH = 16
ITERS = 3


def from_behind(value, axis, steps):
    count = lax.axis_size(axis)
    first, last = (max(0, -steps), min(count, count - steps))
    return lax.ppermute(value, axis, [(source, source + steps) for source in range(first, last)])


def small_solve(gram, target):
    size = gram.shape[0]
    factor = {}
    for block_position in range(size):
        running = gram[block_position, block_position]
        for k in range(block_position):
            running = running - factor[block_position, k] * factor[block_position, k]
        factor[block_position, block_position] = jnp.sqrt(running)
        for i in range(block_position + 1, size):
            running = gram[i, block_position]
            for k in range(block_position):
                running = running - factor[i, k] * factor[block_position, k]
            factor[i, block_position] = running / factor[block_position, block_position]
    forward = []
    for i in range(size):
        running = target[i]
        for k in range(i):
            running = running - factor[i, k] * forward[k]
        forward.append(running / factor[i, i])
    analysis_output = [None] * size
    for i in reversed(range(size)):
        running = forward[i]
        for k in range(i + 1, size):
            running = running - factor[k, i] * analysis_output[k]
        analysis_output[i] = running / factor[i, i]
    return jnp.stack(analysis_output)


def previous_blocks(entry_values, reach_devices):
    pieces = [
        from_behind(entry_values, ("region", "blk"), shift_by)
        for shift_by in range(reach_devices, 0, -1)
    ]
    return jnp.concatenate(pieces, axis=0)


def on_device(ensemble, observed, obs_var, ridge, pred_back, bounds):
    highest = lax.Precision.HIGHEST
    local_blocks, rows, members = ensemble.shape
    slots = pred_back.shape[1]
    reach_devices = -(-REACH // local_blocks)
    before = reach_devices * local_blocks
    anomaly = (ensemble - jnp.mean(ensemble, axis=2, keepdims=True)) / jnp.sqrt(
        jnp.float32(members - 1)
    )
    positions = before + jnp.arange(local_blocks, dtype=jnp.int32)[:, None] - pred_back
    positions = jnp.where(pred_back > 0, positions, before + local_blocks)
    empty_zero_matrix = jnp.zeros((1, rows, members), jnp.float32)

    def extend(entry_values):
        return jnp.concatenate(
            [previous_blocks(entry_values, reach_devices), entry_values, empty_zero_matrix], axis=0
        )

    preds = extend(anomaly)[positions]
    identity = jnp.eye(slots, dtype=jnp.float32)
    gram = jnp.einsum("bjrm,bkrm->jkbr", preds, preds, precision=highest)
    gram = gram + ridge[None, None, :, None] * identity[:, :, None, None]
    target = jnp.einsum("bjrm,brm->jbr", preds, anomaly, precision=highest)
    regression_coefficients = small_solve(gram, target)
    resid = anomaly - jnp.einsum("jbr,bjrm->brm", regression_coefficients, preds, precision=highest)
    inverse_var = 1.0 / (jnp.sum(resid * resid, axis=2) + 1e-05)
    inverse_obs = 1.0 / obs_var
    beta_blocks = jnp.transpose(regression_coefficients, (1, 0, 2))
    lower_bound = bounds[0]
    upper_bound = bounds[1]
    theta = (upper_bound + lower_bound) / 2
    delta = (upper_bound - lower_bound) / 2
    sigma = theta / delta
    rho_now = 1.0 / sigma
    residue = inverse_obs[:, :, None] * (observed - ensemble)
    increment = jnp.zeros_like(ensemble)
    direction = residue / theta
    for step in range(ITERS):
        increment = increment + direction
        extended = extend(direction)
        lower_analysis_output = direction
        for lower_slot in range(slots):
            lower_analysis_output = (
                lower_analysis_output
                - beta_blocks[:, lower_slot, :, None] * extended[positions[:, lower_slot]]
            )
        upper_entry_values = lower_analysis_output * inverse_var[:, :, None]
        window = jnp.zeros((before + local_blocks + 1, rows, members), jnp.float32)
        for slot in range(slots):
            window = window.at[positions[:, slot]].add(
                beta_blocks[:, slot, :, None] * upper_entry_values
            )
        analysis_output = upper_entry_values - window[before : before + local_blocks]
        for shift_by in range(1, reach_devices + 1):
            start = (reach_devices - shift_by) * local_blocks
            analysis_output = analysis_output - from_behind(
                window[start : start + local_blocks], ("region", "blk"), -shift_by
            )
        residue = residue - (analysis_output + inverse_obs[:, :, None] * direction)
        rho_next = 1.0 / (2 * sigma - rho_now)
        direction = rho_next * rho_now * direction + 2 * rho_next / delta * residue
        rho_now = rho_next
    increment = increment + direction
    return ensemble + increment


def solution(mesh):
    return jax.shard_map(
        on_device,
        mesh=mesh,
        in_specs=(
            P(("region", "blk"), None, None),
            P(("region", "blk"), None, None),
            P(("region", "blk"), None),
            P(("region", "blk")),
            P(("region", "blk"), None),
            P(),
        ),
        out_specs=P(("region", "blk"), None, None),
        check_vma=False,
    )
```

profile of v0, /device:TPU:136, one launch (start us, length us, event | category | flops | bytes accessed | tf_op | source)
XLA Modules:
  0.0 737.2 jit_solution(6091333086175009796)
XLA Ops:
  16.7 4.9 collective-permute-start.3
  21.6 4.6 collective-permute-start.4
  57.8 4.9 collective-permute-start.12
  67.3 9.3 %bitcast_add_fusion = f32[12,12,2,256]{0,1,3,2:T(8,128)} fusion(f32[2,12,256,128]{3,2,1,0:T(8,128)S(1)} %bitcast.1005, f32[12,12,2]{0,1,2:T(8,128)S(1)} %broadcast_multiply_fusion.36), kind=kOutput, calls=%fused_computation.79 | convolution fusion | flops 113319936 | bytes 3441792 | tf_op jit(solution)/shard_map/bjrm,bkrm->jkbr/dot_general | solution.py:72
  76.6 64.5 %slice_reduce_fusion.56 = (f32[2,256]{1,0:T(2,128)}, f32[2,256]{1,0:T(2,128)}, f32[2,256]{1,0:T(2,128)}, f32[2,256]{1,0:T(2,128)}, f32[2,256]{1,0:T(2,128)S(1)},...) fusion(f32[12,12,2,256]{0,1,3,2:T(8,128)} %bitcast_add_fusion), kind=kLoop, calls=%fused_computation.173 | loop fusion | bytes 77824 | tf_op jit(solution)/shard_map/slice | solution.py:25
  141.1 50.0 %rsqrt_reduce_fusion = (f32[2,256]{1,0:T(2,128)S(1)}, f32[2,256]{1,0:T(2,128)}, f32[2,256]{1,0:T(2,128)}, f32[2,256]{1,0:T(2,128)}, f32[2,256]{1,0:T(2,128)}, /*...) fusion(f32[12,12,2,256]{0,1,3,2:T(8,128)} %bitcast_add_fusion), kind=kLoop, calls=%fused_computation.200 | loop fusion | bytes 77824 | tf_op jit(solution)/shard_map/sqrt | solution.py:23
  191.1 8.5 %slice_reduce_fusion.75 = (f32[2,256]{1,0:T(2,128)S(1)}, f32[2,256]{1,0:T(2,128)S(1)}, f32[2,256]{1,0:T(2,128)S(1)}) fusion(f32[12,12,2,256]{0,1,3,2:T(8,128)} %bitcast_add_fusion), kind=kLoop, calls=%fused_computation.192 | loop fusion | bytes 12288 | tf_op jit(solution)/shard_map/slice | solution.py:20
  199.7 55.6 %slice_reduce_fusion.42 = (f32[2,256]{1,0:T(2,128)}, f32[2,256]{1,0:T(2,128)}, f32[2,256]{1,0:T(2,128)}, f32[2,256]{1,0:T(2,128)S(1)}, f32[2,256]{1,0:T(2,128)S(...) fusion(f32[12,12,2,256]{0,1,3,2:T(8,128)} %bitcast_add_fusion), kind=kLoop, calls=%fused_computation.159 | loop fusion | bytes 77824 | tf_op jit(solution)/shard_map/slice | solution.py:20
  255.3 51.0 %slice_reduce_fusion.23 = (f32[2,256]{1,0:T(2,128)}, f32[2,256]{1,0:T(2,128)}, f32[2,256]{1,0:T(2,128)}, f32[2,256]{1,0:T(2,128)S(1)}, f32[2,256]{1,0:T(2,128)S(...) fusion(f32[12,12,2,256]{0,1,3,2:T(8,128)} %bitcast_add_fusion), kind=kLoop, calls=%fused_computation.140 | loop fusion | bytes 77824 | tf_op jit(solution)/shard_map/slice | solution.py:20
  306.3 9.5 %fusion.2 = f32[2,256,1,12]{3,2,1,0:T(1,128)} fusion(f32[2,256,128,1]{2,3,1,0:T(1,128)} %bitcast.1008, f32[2,12,256,128]{3,2,1,0:T(8,128)S(1)} %bitcast.1006), kind=kOutput, calls=%fused_computation.75 | convolution fusion | flops 9437184 | bytes 3432448 | tf_op jit(solution)/shard_map/bjrm,brm->jbr/dot_general | solution.py:74
  328.0 6.5 fusion
  347.2 6.2 collective-permute-done.14
  400.8 7.4 %collective-permute-start.19 = (f32[2,256,128]{2,1,0:T(8,128)}, f32[2,256,128]{2,1,0:T(8,128)}, u32[]{:S(2)}, u32[]{:S(2)}) collective-permute-start(f32[2,256,128]{2,1,0:T(8,128)} %get-tuple-element.302), channel_id=1, source_target_pairs={{4,0},{5,1},{6,2},{7,3},{8,4},{9,5},{10,6},{11,7},{12,8},{13,9},{1... | collective-permute-start | bytes 786440 | tf_op jit(solution)/shard_map/ppermute | solution.py:13
  417.5 8.5 %collective-permute-start.23 = (f32[2,256,128]{2,1,0:T(8,128)}, f32[2,256,128]{2,1,0:T(8,128)}, u32[]{:S(2)}, u32[]{:S(2)}) collective-permute-start(f32[2,256,128]{2,1,0:T(8,128)} %get-tuple-element.298), channel_id=1, source_target_pairs={{8,0},{9,1},{10,2},{11,3},{12,4},{13,5},{14,6},{15,7},{16,8},{17,9... | collective-permute-start | bytes 786440 | tf_op jit(solution)/shard_map/ppermute | solution.py:13
  430.4 5.6 collective-permute-done.21
  436.0 5.6 collective-permute-done.22
  441.6 7.1 collective-permute-done.23
  457.8 5.8 collective-permute-start.27
  475.5 4.9 collective-permute-done.28
  483.5 9.6 %collective-permute-done.30 = f32[2,256,128]{2,1,0:T(8,128)S(1)} collective-permute-done((f32[2,256,128]{2,1,0:T(8,128)S(1)}, f32[2,256,128]{2,1,0:T(8,128)S(1)}, u32[]{:S(2)}, u32[]{:S(2)}) %collective-permute-start.30) | collective-permute-done | bytes 262176 | tf_op jit(solution)/shard_map/ppermute | solution.py:13
  544.3 5.7 collective-permute-start.35
  560.0 7.3 collective-permute-start.39
  575.7 5.6 collective-permute-done.38
  581.3 9.3 %collective-permute-done.39 = f32[2,256,128]{2,1,0:T(8,128)} collective-permute-done((f32[2,256,128]{2,1,0:T(8,128)}, f32[2,256,128]{2,1,0:T(8,128)}, u32[]{:S(2)}, u32[]{:S(2)}) %collective-permute-start.39) | collective-permute-done | bytes 262176 | tf_op jit(solution)/shard_map/ppermute | solution.py:13
  598.9 8.2 %collective-permute-start.43 = (f32[2,256,128]{2,1,0:T(8,128)S(1)}, f32[2,256,128]{2,1,0:T(8,128)S(1)}, u32[]{:S(2)}, u32[]{:S(2)}) collective-permute-start(f32[2,256,128]{2,1,0:T(8,128)S(1)} %get-tuple-element.98), channel_id=1, source_target_pairs={{0,5},{1,6},{2,7},{3,8},{4,9},{5,10},{6,11},{7,12},{8,13},{9,14},{... | collective-permute-start | bytes 786440 | tf_op jit(solution)/shard_map/ppermute | solution.py:13
  607.1 4.8 collective-permute-start.44
  624.3 11.4 %collective-permute-done.46 = f32[2,256,128]{2,1,0:T(8,128)S(1)} collective-permute-done((f32[2,256,128]{2,1,0:T(8,128)S(1)}, f32[2,256,128]{2,1,0:T(8,128)S(1)}, u32[]{:S(2)}, u32[]{:S(2)}) %collective-permute-start.46) | collective-permute-done | bytes 262176 | tf_op jit(solution)/shard_map/ppermute | solution.py:13
  685.4 6.4 collective-permute-start.51
  708.9 6.4 collective-permute-done.52
  715.2 5.6 collective-permute-done.53
  720.8 5.6 collective-permute-done.54
  726.4 7.7 %collective-permute-done.55 = f32[2,256,128]{2,1,0:T(8,128)} collective-permute-done((f32[2,256,128]{2,1,0:T(8,128)}, f32[2,256,128]{2,1,0:T(8,128)}, u32[]{:S(2)}, u32[]{:S(2)}) %collective-permute-start.55) | collective-permute-done | bytes 262176 | tf_op jit(solution)/shard_map/ppermute | solution.py:13
  (333 shorter events, 318.1 us)
Async XLA Ops:
  5.6 26.4 %collective-permute-start = (f32[2,256,128]{2,1,0:T(8,128)S(1)}, f32[2,256,128]{2,1,0:T(8,128)S(1)}, u32[]{:S(2)}, u32[]{:S(2)}) collective-permute-start(f32[2,256,128]{2,1,0:T(8,128)S(1)} %get-tuple-element.338), channel_id=1, source_target_pairs={{0,8},{1,9},{2,10},{3,11},{4,12},{5,13},{6,14},{7,15},{8,16},{9,17... | collective-permute-start | bytes 786440 | tf_op jit(solution)/shard_map/ppermute | solution.py:13
  9.1 25.6 %collective-permute-start.1 = (f32[2,256,128]{2,1,0:T(8,128)S(1)}, f32[2,256,128]{2,1,0:T(8,128)S(1)}, u32[]{:S(2)}, u32[]{:S(2)}) collective-permute-start(f32[2,256,128]{2,1,0:T(8,128)S(1)} %get-tuple-element.338), channel_id=1, source_target_pairs={{0,7},{1,8},{2,9},{3,10},{4,11},{5,12},{6,13},{7,14},{8,15},{9,16}... | collective-permute-start | bytes 786440 | tf_op jit(solution)/shard_map/ppermute | solution.py:13
  12.9 24.6 %collective-permute-start.2 = (f32[2,256,128]{2,1,0:T(8,128)S(1)}, f32[2,256,128]{2,1,0:T(8,128)S(1)}, u32[]{:S(2)}, u32[]{:S(2)}) collective-permute-start(f32[2,256,128]{2,1,0:T(8,128)S(1)} %get-tuple-element.338), channel_id=1, source_target_pairs={{0,6},{1,7},{2,8},{3,9},{4,10},{5,11},{6,12},{7,13},{8,14},{9,15},... | collective-permute-start | bytes 786440 | tf_op jit(solution)/shard_map/ppermute | solution.py:13
  16.7 24.9 %collective-permute-start.3 = (f32[2,256,128]{2,1,0:T(8,128)S(1)}, f32[2,256,128]{2,1,0:T(8,128)S(1)}, u32[]{:S(2)}, u32[]{:S(2)}) collective-permute-start(f32[2,256,128]{2,1,0:T(8,128)S(1)} %get-tuple-element.338), channel_id=1, source_target_pairs={{0,5},{1,6},{2,7},{3,8},{4,9},{5,10},{6,11},{7,12},{8,13},{9,14},{... | collective-permute-start | bytes 786440 | tf_op jit(solution)/shard_map/ppermute | solution.py:13
  21.6 23.2 %collective-permute-start.4 = (f32[2,256,128]{2,1,0:T(8,128)S(1)}, f32[2,256,128]{2,1,0:T(8,128)S(1)}, u32[]{:S(2)}, u32[]{:S(2)}) collective-permute-start(f32[2,256,128]{2,1,0:T(8,128)S(1)} %get-tuple-element.338), channel_id=1, source_target_pairs={{0,4},{1,5},{2,6},{3,7},{4,8},{5,9},{6,10},{7,11},{8,12},{9,13},{1... | collective-permute-start | bytes 786440 | tf_op jit(solution)/shard_map/ppermute | solution.py:13
  37.5 20.3 %collective-permute-start.7 = (f32[2,256,128]{2,1,0:T(8,128)S(1)}, f32[2,256,128]{2,1,0:T(8,128)S(1)}, u32[]{:S(2)}, u32[]{:S(2)}) collective-permute-start(f32[2,256,128]{2,1,0:T(8,128)S(1)} %get-tuple-element.338), channel_id=1, source_target_pairs={{0,1},{1,2},{2,3},{3,4},{4,5},{5,6},{6,7},{7,8},{8,9},{9,10},{10,1... | collective-permute-start | bytes 786440 | tf_op jit(solution)/shard_map/ppermute | solution.py:13
  41.5 293.0 %collective-permute-start.8 = (f32[2,256,128]{2,1,0:T(8,128)S(1)}, f32[2,256,128]{2,1,0:T(8,128)}, u32[]{:S(2)}, u32[]{:S(2)}) collective-permute-start(f32[2,256,128]{2,1,0:T(8,128)S(1)} %get-tuple-element.339), channel_id=1, source_target_pairs={{0,8},{1,9},{2,10},{3,11},{4,12},{5,13},{6,14},{7,15},{8,16},{9,17... | collective-permute-start | bytes 786440 | tf_op jit(solution)/shard_map/ppermute | solution.py:13
  44.8 292.7 %collective-permute-start.9 = (f32[2,256,128]{2,1,0:T(8,128)S(1)}, f32[2,256,128]{2,1,0:T(8,128)}, u32[]{:S(2)}, u32[]{:S(2)}) collective-permute-start(f32[2,256,128]{2,1,0:T(8,128)S(1)} %get-tuple-element.339), channel_id=1, source_target_pairs={{0,7},{1,8},{2,9},{3,10},{4,11},{5,12},{6,13},{7,14},{8,15},{9,16}... | collective-permute-start | bytes 786440 | tf_op jit(solution)/shard_map/ppermute | solution.py:13
  49.3 292.6 %collective-permute-start.10 = (f32[2,256,128]{2,1,0:T(8,128)S(1)}, f32[2,256,128]{2,1,0:T(8,128)}, u32[]{:S(2)}, u32[]{:S(2)}) collective-permute-start(f32[2,256,128]{2,1,0:T(8,128)S(1)} %get-tuple-element.339), channel_id=1, source_target_pairs={{0,6},{1,7},{2,8},{3,9},{4,10},{5,11},{6,12},{7,13},{8,14},{9,15},... | collective-permute-start | bytes 786440 | tf_op jit(solution)/shard_map/ppermute | solution.py:13
  53.4 291.6 %collective-permute-start.11 = (f32[2,256,128]{2,1,0:T(8,128)S(1)}, f32[2,256,128]{2,1,0:T(8,128)}, u32[]{:S(2)}, u32[]{:S(2)}) collective-permute-start(f32[2,256,128]{2,1,0:T(8,128)S(1)} %get-tuple-element.339), channel_id=1, source_target_pairs={{0,5},{1,6},{2,7},{3,8},{4,9},{5,10},{6,11},{7,12},{8,13},{9,14},{... | collective-permute-start | bytes 786440 | tf_op jit(solution)/shard_map/ppermute | solution.py:13
  57.8 288.2 %collective-permute-start.12 = (f32[2,256,128]{2,1,0:T(8,128)S(1)}, f32[2,256,128]{2,1,0:T(8,128)}, u32[]{:S(2)}, u32[]{:S(2)}) collective-permute-start(f32[2,256,128]{2,1,0:T(8,128)S(1)} %get-tuple-element.339), channel_id=1, source_target_pairs={{0,4},{1,5},{2,6},{3,7},{4,8},{5,9},{6,10},{7,11},{8,12},{9,13},{1... | collective-permute-start | bytes 786440 | tf_op jit(solution)/shard_map/ppermute | solution.py:13
  400.8 26.6 %collective-permute-start.19 = (f32[2,256,128]{2,1,0:T(8,128)}, f32[2,256,128]{2,1,0:T(8,128)}, u32[]{:S(2)}, u32[]{:S(2)}) collective-permute-start(f32[2,256,128]{2,1,0:T(8,128)} %get-tuple-element.302), channel_id=1, source_target_pairs={{4,0},{5,1},{6,2},{7,3},{8,4},{9,5},{10,6},{11,7},{12,8},{13,9},{1... | collective-permute-start | bytes 786440 | tf_op jit(solution)/shard_map/ppermute | solution.py:13
  408.2 22.2 %collective-permute-start.20 = (f32[2,256,128]{2,1,0:T(8,128)}, f32[2,256,128]{2,1,0:T(8,128)}, u32[]{:S(2)}, u32[]{:S(2)}) collective-permute-start(f32[2,256,128]{2,1,0:T(8,128)} %get-tuple-element.301), channel_id=1, source_target_pairs={{5,0},{6,1},{7,2},{8,3},{9,4},{10,5},{11,6},{12,7},{13,8},{14,9},{... | collective-permute-start | bytes 786440 | tf_op jit(solution)/shard_map/ppermute | solution.py:13
  410.2 25.8 %collective-permute-start.21 = (f32[2,256,128]{2,1,0:T(8,128)}, f32[2,256,128]{2,1,0:T(8,128)}, u32[]{:S(2)}, u32[]{:S(2)}) collective-permute-start(f32[2,256,128]{2,1,0:T(8,128)} %get-tuple-element.300), channel_id=1, source_target_pairs={{6,0},{7,1},{8,2},{9,3},{10,4},{11,5},{12,6},{13,7},{14,8},{15,9},... | collective-permute-start | bytes 786440 | tf_op jit(solution)/shard_map/ppermute | solution.py:13
  413.8 27.9 %collective-permute-start.22 = (f32[2,256,128]{2,1,0:T(8,128)}, f32[2,256,128]{2,1,0:T(8,128)}, u32[]{:S(2)}, u32[]{:S(2)}) collective-permute-start(f32[2,256,128]{2,1,0:T(8,128)} %get-tuple-element.299), channel_id=1, source_target_pairs={{7,0},{8,1},{9,2},{10,3},{11,4},{12,5},{13,6},{14,7},{15,8},{16,9}... | collective-permute-start | bytes 786440 | tf_op jit(solution)/shard_map/ppermute | solution.py:13
  417.5 31.2 %collective-permute-start.23 = (f32[2,256,128]{2,1,0:T(8,128)}, f32[2,256,128]{2,1,0:T(8,128)}, u32[]{:S(2)}, u32[]{:S(2)}) collective-permute-start(f32[2,256,128]{2,1,0:T(8,128)} %get-tuple-element.298), channel_id=1, source_target_pairs={{8,0},{9,1},{10,2},{11,3},{12,4},{13,5},{14,6},{15,7},{16,8},{17,9... | collective-permute-start | bytes 786440 | tf_op jit(solution)/shard_map/ppermute | solution.py:13
  469.6 23.4 %collective-permute-start.30 = (f32[2,256,128]{2,1,0:T(8,128)S(1)}, f32[2,256,128]{2,1,0:T(8,128)S(1)}, u32[]{:S(2)}, u32[]{:S(2)}) collective-permute-start(f32[2,256,128]{2,1,0:T(8,128)S(1)} %get-tuple-element.102), channel_id=1, source_target_pairs={{0,2},{1,3},{2,4},{3,5},{4,6},{5,7},{6,8},{7,9},{8,10},{9,11},{10,... | collective-permute-start | bytes 786440 | tf_op jit(solution)/shard_map/ppermute | solution.py:13
  473.5 20.4 %collective-permute-start.31 = (f32[2,256,128]{2,1,0:T(8,128)S(1)}, f32[2,256,128]{2,1,0:T(8,128)S(1)}, u32[]{:S(2)}, u32[]{:S(2)}) collective-permute-start(f32[2,256,128]{2,1,0:T(8,128)S(1)} %get-tuple-element.102), channel_id=1, source_target_pairs={{0,1},{1,2},{2,3},{3,4},{4,5},{5,6},{6,7},{7,8},{8,9},{9,10},{10,1... | collective-permute-start | bytes 786440 | tf_op jit(solution)/shard_map/ppermute | solution.py:13
  544.3 23.3 %collective-permute-start.35 = (f32[2,256,128]{2,1,0:T(8,128)}, f32[2,256,128]{2,1,0:T(8,128)}, u32[]{:S(2)}, u32[]{:S(2)}) collective-permute-start(f32[2,256,128]{2,1,0:T(8,128)} %get-tuple-element.294), channel_id=1, source_target_pairs={{4,0},{5,1},{6,2},{7,3},{8,4},{9,5},{10,6},{11,7},{12,8},{13,9},{1... | collective-permute-start | bytes 786440 | tf_op jit(solution)/shard_map/ppermute | solution.py:13
  550.0 21.1 %collective-permute-start.36 = (f32[2,256,128]{2,1,0:T(8,128)}, f32[2,256,128]{2,1,0:T(8,128)}, u32[]{:S(2)}, u32[]{:S(2)}) collective-permute-start(f32[2,256,128]{2,1,0:T(8,128)} %get-tuple-element.293), channel_id=1, source_target_pairs={{5,0},{6,1},{7,2},{8,3},{9,4},{10,5},{11,6},{12,7},{13,8},{14,9},{... | collective-permute-start | bytes 786440 | tf_op jit(solution)/shard_map/ppermute | solution.py:13
  552.0 23.7 %collective-permute-start.37 = (f32[2,256,128]{2,1,0:T(8,128)}, f32[2,256,128]{2,1,0:T(8,128)}, u32[]{:S(2)}, u32[]{:S(2)}) collective-permute-start(f32[2,256,128]{2,1,0:T(8,128)} %get-tuple-element.292), channel_id=1, source_target_pairs={{6,0},{7,1},{8,2},{9,3},{10,4},{11,5},{12,6},{13,7},{14,8},{15,9},... | collective-permute-start | bytes 786440 | tf_op jit(solution)/shard_map/ppermute | solution.py:13
  555.5 25.8 %collective-permute-start.38 = (f32[2,256,128]{2,1,0:T(8,128)}, f32[2,256,128]{2,1,0:T(8,128)}, u32[]{:S(2)}, u32[]{:S(2)}) collective-permute-start(f32[2,256,128]{2,1,0:T(8,128)} %get-tuple-element.291), channel_id=1, source_target_pairs={{7,0},{8,1},{9,2},{10,3},{11,4},{12,5},{13,6},{14,7},{15,8},{16,9}... | collective-permute-start | bytes 786440 | tf_op jit(solution)/shard_map/ppermute | solution.py:13
  560.0 30.6 %collective-permute-start.39 = (f32[2,256,128]{2,1,0:T(8,128)}, f32[2,256,128]{2,1,0:T(8,128)}, u32[]{:S(2)}, u32[]{:S(2)}) collective-permute-start(f32[2,256,128]{2,1,0:T(8,128)} %get-tuple-element.290), channel_id=1, source_target_pairs={{8,0},{9,1},{10,2},{11,3},{12,4},{13,5},{14,6},{15,7},{16,8},{17,9... | collective-permute-start | bytes 786440 | tf_op jit(solution)/shard_map/ppermute | solution.py:13
  597.0 20.1 %collective-permute-start.42 = (f32[2,256,128]{2,1,0:T(8,128)S(1)}, f32[2,256,128]{2,1,0:T(8,128)S(1)}, u32[]{:S(2)}, u32[]{:S(2)}) collective-permute-start(f32[2,256,128]{2,1,0:T(8,128)S(1)} %get-tuple-element.98), channel_id=1, source_target_pairs={{0,6},{1,7},{2,8},{3,9},{4,10},{5,11},{6,12},{7,13},{8,14},{9,15},... | collective-permute-start | bytes 786440 | tf_op jit(solution)/shard_map/ppermute | solution.py:13
  598.9 20.5 %collective-permute-start.43 = (f32[2,256,128]{2,1,0:T(8,128)S(1)}, f32[2,256,128]{2,1,0:T(8,128)S(1)}, u32[]{:S(2)}, u32[]{:S(2)}) collective-permute-start(f32[2,256,128]{2,1,0:T(8,128)S(1)} %get-tuple-element.98), channel_id=1, source_target_pairs={{0,5},{1,6},{2,7},{3,8},{4,9},{5,10},{6,11},{7,12},{8,13},{9,14},{... | collective-permute-start | bytes 786440 | tf_op jit(solution)/shard_map/ppermute | solution.py:13
  613.9 21.7 %collective-permute-start.46 = (f32[2,256,128]{2,1,0:T(8,128)S(1)}, f32[2,256,128]{2,1,0:T(8,128)S(1)}, u32[]{:S(2)}, u32[]{:S(2)}) collective-permute-start(f32[2,256,128]{2,1,0:T(8,128)S(1)} %get-tuple-element.98), channel_id=1, source_target_pairs={{0,2},{1,3},{2,4},{3,5},{4,6},{5,7},{6,8},{7,9},{8,10},{9,11},{10,... | collective-permute-start | bytes 786440 | tf_op jit(solution)/shard_map/ppermute | solution.py:13
  617.1 19.4 %collective-permute-start.47 = (f32[2,256,128]{2,1,0:T(8,128)S(1)}, f32[2,256,128]{2,1,0:T(8,128)S(1)}, u32[]{:S(2)}, u32[]{:S(2)}) collective-permute-start(f32[2,256,128]{2,1,0:T(8,128)S(1)} %get-tuple-element.98), channel_id=1, source_target_pairs={{0,1},{1,2},{2,3},{3,4},{4,5},{5,6},{6,7},{7,8},{8,9},{9,10},{10,1... | collective-permute-start | bytes 786440 | tf_op jit(solution)/shard_map/ppermute | solution.py:13
  685.4 23.5 %collective-permute-start.51 = (f32[2,256,128]{2,1,0:T(8,128)}, f32[2,256,128]{2,1,0:T(8,128)}, u32[]{:S(2)}, u32[]{:S(2)}) collective-permute-start(f32[2,256,128]{2,1,0:T(8,128)} %get-tuple-element.286), channel_id=1, source_target_pairs={{4,0},{5,1},{6,2},{7,3},{8,4},{9,5},{10,6},{11,7},{12,8},{13,9},{1... | collective-permute-start | bytes 786440 | tf_op jit(solution)/shard_map/ppermute | solution.py:13
  691.8 23.4 %collective-permute-start.52 = (f32[2,256,128]{2,1,0:T(8,128)}, f32[2,256,128]{2,1,0:T(8,128)}, u32[]{:S(2)}, u32[]{:S(2)}) collective-permute-start(f32[2,256,128]{2,1,0:T(8,128)} %get-tuple-element.285), channel_id=1, source_target_pairs={{5,0},{6,1},{7,2},{8,3},{9,4},{10,5},{11,6},{12,7},{13,8},{14,9},{... | collective-permute-start | bytes 786440 | tf_op jit(solution)/shard_map/ppermute | solution.py:13
  693.8 27.1 %collective-permute-start.53 = (f32[2,256,128]{2,1,0:T(8,128)}, f32[2,256,128]{2,1,0:T(8,128)}, u32[]{:S(2)}, u32[]{:S(2)}) collective-permute-start(f32[2,256,128]{2,1,0:T(8,128)} %get-tuple-element.284), channel_id=1, source_target_pairs={{6,0},{7,1},{8,2},{9,3},{10,4},{11,5},{12,6},{13,7},{14,8},{15,9},... | collective-permute-start | bytes 786440 | tf_op jit(solution)/shard_map/ppermute | solution.py:13
  697.2 29.2 %collective-permute-start.54 = (f32[2,256,128]{2,1,0:T(8,128)}, f32[2,256,128]{2,1,0:T(8,128)}, u32[]{:S(2)}, u32[]{:S(2)}) collective-permute-start(f32[2,256,128]{2,1,0:T(8,128)} %get-tuple-element.283), channel_id=1, source_target_pairs={{7,0},{8,1},{9,2},{10,3},{11,4},{12,5},{13,6},{14,7},{15,8},{16,9}... | collective-permute-start | bytes 786440 | tf_op jit(solution)/shard_map/ppermute | solution.py:13
  701.4 32.7 %collective-permute-start.55 = (f32[2,256,128]{2,1,0:T(8,128)}, f32[2,256,128]{2,1,0:T(8,128)}, u32[]{:S(2)}, u32[]{:S(2)}) collective-permute-start(f32[2,256,128]{2,1,0:T(8,128)} %get-tuple-element.282), channel_id=1, source_target_pairs={{8,0},{9,1},{10,2},{11,3},{12,4},{13,5},{14,6},{15,7},{16,8},{17,9... | collective-permute-start | bytes 786440 | tf_op jit(solution)/shard_map/ppermute | solution.py:13
  (60 other events, 1009.9 us)
where the time goes:
time: 746 us; the launch traced here: 737 us
  local copies, waits for them, and re-layouts  302 us (40%)
  starting transfers between devices  188 us (25%)
  waiting for transfers between devices  120 us (16%)
  other arithmetic  98 us (13%)
  matrix products  25.3 us (3%)
    ppermute x56, starting transfers between devices, from_behind(): lax.ppermute(value, axis, [(source, source + steps) for source in range(f...  188 us
    ppermute x56, waiting for transfers between devices, from_behind(): lax.ppermute(value, axis, [(source, source + steps) for source in range(f...  120 us
    slice x3, local copies, waits for them, and re-layouts, small_solve(): running = gram[block_position, block_position]  115 us
    slice x1, local copies, waits for them, and re-layouts, small_solve(): running = gram[i, block_position]  64.5 us
    scatter-add x36, other arithmetic, on_device(): window.at[positions[:, slot]]  55.9 us
    sqrt x1, local copies, waits for them, and re-layouts, small_solve(): factor[block_position, block_position] = jnp.sqrt(running)  50 us
    gather x36, local copies, waits for them, and re-layouts, on_device(): extended[positions[:, lower_slot]]  48.7 us
    mul x6, other arithmetic, on_device(): beta_blocks[:, slot, :, None] * upper_entry_values  15.6 us
  transfers between devices with their start and end apart: 56, of which 27 were waited for; matrix products, arithmetic and copies ran while one was open for 39% of the time, Pallas kernels for 0%

commit v1 on v0

v1 whole, which is shorter than its diff:
```python
import jax
import jax.numpy as jnp
from jax import lax
from jax.experimental import pallas as pl
from jax.experimental.pallas import tpu as pltpu
from jax.sharding import PartitionSpec as P

REACH = 16
ITERS = 3
HALO = ITERS * REACH
AXES = ("region", "blk")
LANES = 128
SPAN = 256
CHUNK = 17
META = 16
HIGHEST = lax.Precision.HIGHEST
PARAMS = pltpu.CompilerParams(vmem_limit_bytes=48 * 1024 * 1024)


def iota(shape, axis):
    return lax.broadcasted_iota(jnp.int32, shape, axis)


def pack_kernel(pred_ref, ridge_ref, ens_ref, obs_ref, var_ref, out_ref):
    local_blocks, rows, members = ens_ref.shape
    slots = pred_ref.shape[1]
    last = members - 1
    groups = rows // 8
    low = iota((groups, 8, members), 1) < 4
    lane = iota((rows, members), 1)
    spot = iota((1, members), 1)
    meta = jnp.zeros((1, members), jnp.float32)
    for b in range(local_blocks):
        for k in range(slots):
            meta = jnp.where(spot == META * b + k, pred_ref[b, k].astype(jnp.float32), meta)
        meta = jnp.where(spot == META * b + slots, ridge_ref[b], meta)
        ens = ens_ref[b]
        anomaly = (ens - jnp.mean(ens, axis=1, keepdims=True)) * (1.0 / (members - 1) ** 0.5)
        folded = anomaly + anomaly[:, last:] * (1.0 / (members**0.5 - 1.0))
        variance = jnp.broadcast_to(var_ref[b : b + 1, :], (members, rows)).T
        first = jnp.where(lane == last, variance, folded).reshape(groups, 8, members)
        second = (obs_ref[b] - ens).reshape(groups, 8, members)
        even = jnp.where(low, first, pltpu.roll(second, 4, 1))
        odd = jnp.where(low, pltpu.roll(first, 4, 1), second)
        for q in range(groups):
            at = 2 * q * CHUNK + 8 * b
            out_ref[at : at + 8, :] = even[q]
            out_ref[at + CHUNK : at + CHUNK + 8, :] = odd[q]
    for p in range(2 * groups):
        out_ref[p * CHUNK + CHUNK - 1 : (p + 1) * CHUNK, :] = meta


def add_kernel(ens_ref, inc_ref, out_ref):
    groups, _, _, members = inc_ref.shape
    low = iota((groups, 8, members), 1) < 4
    even, odd = inc_ref[:, 0], inc_ref[:, 1]
    shape = ens_ref.shape[1:]
    out_ref[0] = ens_ref[0] + jnp.where(low, even, pltpu.roll(odd, 4, 1)).reshape(shape)
    out_ref[1] = ens_ref[1] + jnp.where(low, pltpu.roll(even, 4, 1), odd).reshape(shape)


def solve_lags(gram, target):
    size = len(target)
    factor = {}
    inverse = []
    for j in range(size):
        for i in range(j, size):
            running = gram[i, j]
            for k in range(j):
                running = running - factor[i, k] * factor[j, k]
            if i == j:
                inverse.append(lax.rsqrt(running))
            else:
                factor[i, j] = running * inverse[j]
    forward = []
    for i in range(size):
        running = target[i]
        for k in range(i):
            running = running - factor[i, k] * forward[k]
        forward.append(running * inverse[i])
    beta = [None] * size
    for i in reversed(range(size)):
        running = forward[i]
        for k in range(i + 1, size):
            running = running - factor[k, i] * beta[k]
        beta[i] = running * inverse[i]
    return beta


def main_kernel(
    bounds_ref, own_ref, before_ref, after_ref, out_ref,
    tile_ref, x_ref, res_ref, dir_ref, inc_ref, exact_ref, high_ref, low_ref, sums_ref, beta_ref, meta_ref,
):
    rows = 4
    slots = 12
    members = LANES
    sources = [before_ref, own_ref, after_ref]
    counts = [ref.shape[0] // CHUNK for ref in sources]
    blocks = 2 * counts[1]
    chunks = sum(counts)
    at = 0
    for ref, count in zip(sources, counts):
        for s in range(count):
            tile_ref[at : at + 16, :] = ref[s * CHUNK : s * CHUNK + 16, :]
            at += 16
    tile_ref[at:, :] = jnp.zeros((tile_ref.shape[0] - at, members), jnp.float32)

    def column(offset):
        return tile_ref[pl.ds(offset, SPAN, stride=8), :].T

    facts = [ref[pl.ds(CHUNK - 1, count, stride=CHUNK), :] for ref, count in zip(sources, counts)]
    facts = jnp.concatenate(facts + [jnp.zeros((LANES - chunks, members), jnp.float32)], axis=0).T
    spread = iota((LANES, SPAN), 1) - 2 * iota((LANES, SPAN), 0)
    meta_ref[...] = sum(
        jnp.dot(
            facts[META * b : META * (b + 1), :],
            jnp.where(spread == b, 1.0, 0.0),
            precision=HIGHEST,
            preferred_element_type=jnp.float32,
        )
        for b in range(2)
    )

    lower = jnp.full((1, SPAN), bounds_ref[0], jnp.float32)
    higher = jnp.full((1, SPAN), bounds_ref[1], jnp.float32)
    theta = (higher + lower) / 2
    delta = (higher - lower) / 2
    sigma = theta / delta
    rho = 1.0 / sigma
    keep, gain = [], []
    for _ in range(ITERS):
        rho_next = 1.0 / (2 * sigma - rho)
        keep.append(rho_next * rho)
        gain.append(2 * rho_next / delta)
        rho = rho_next

    member = iota((members, SPAN), 0)
    inverse_obs = []
    for r in range(rows):
        x = column(r)
        variance = x[members - 1 :, :]
        inverse_obs.append(1.0 / jnp.where(variance > 0, variance, 1.0))
        x = jnp.where(member == members - 1, 0.0, x)
        x_ref[r] = x
        res_ref[r] = column(4 + r) * inverse_obs[r]
        for lag in range(REACH + 1):
            other = pltpu.roll(x, lag, 1) if lag else x
            total = jnp.sum(x * other, axis=0, keepdims=True)
            sums_ref[lag, r : r + 1, :] = total[:, :LANES]
            sums_ref[lag, 4 + r : 5 + r, :] = total[:, LANES:]

    upper_half = iota((8, LANES), 0) >= 4
    lane = iota((8, LANES), 1)

    def packed(k):
        return jnp.where(upper_half, meta_ref[k : k + 1, LANES:], meta_ref[k : k + 1, :LANES])

    def shifted(value, lag):
        turned = pltpu.roll(value, lag, 1)
        return jnp.where(lane < lag, pltpu.roll(turned, 4, 0), turned)

    picks = [packed(k) for k in range(slots)]
    ridge = packed(slots)
    used = []
    for lag in range(1, REACH + 1):
        hit = jnp.abs(picks[0] - lag) < 0.5
        for k in range(1, slots):
            hit = hit | (jnp.abs(picks[k] - lag) < 0.5)
        used.append(jnp.where(hit, 1.0, 0.0))
    gram = {}
    for i in range(REACH):
        for j in range(i):
            gram[i, j] = shifted(sums_ref[i - j], j + 1) * (used[i] * used[j])
        gram[i, i] = jnp.where(used[i] > 0, shifted(sums_ref[0], i + 1) + ridge, 1.0)
    target = [sums_ref[i + 1] * used[i] for i in range(REACH)]
    beta = solve_lags(gram, target)
    for i in range(REACH):
        beta_ref[i] = -beta[i]

    for half in range(2):
        start = 0 if half == 0 else LANES - REACH
        stop = LANES * (half + 1)
        shape = (stop - start, LANES)
        lag_of = iota(shape, 1) + half * LANES - iota(shape, 0) - start
        lanes = slice(half * LANES, (half + 1) * LANES)
        for r in range(rows):
            factor = jnp.where(lag_of == 0, 1.0, 0.0)
            for lag in range(1, REACH + 1):
                value = beta_ref[lag - 1, 4 * half + r : 4 * half + r + 1, :]
                factor = jnp.where(lag_of == lag, value, factor)
            high = factor.astype(jnp.bfloat16)
            exact_ref[r, start:stop, lanes] = factor
            high_ref[r, start:stop, lanes] = high
            low_ref[r, start:stop, lanes] = (factor - high.astype(jnp.float32)).astype(jnp.bfloat16)
            rest = slice(stop, SPAN) if half == 0 else slice(0, start)
            empty = (rest.stop - rest.start, LANES)
            exact_ref[r, rest, lanes] = jnp.zeros(empty, jnp.float32)
            high_ref[r, rest, lanes] = jnp.zeros(empty, jnp.bfloat16)
            low_ref[r, rest, lanes] = jnp.zeros(empty, jnp.bfloat16)

    inverse_var = []
    for r in range(rows):
        resid = jnp.dot(
            x_ref[r], exact_ref[r], precision=HIGHEST, preferred_element_type=jnp.float32
        )
        inverse_var.append(1.0 / (jnp.sum(resid * resid, axis=0, keepdims=True) + 1e-05))

    def product(value, r, axis):
        high = value.astype(jnp.bfloat16)
        low = (value - high.astype(jnp.float32)).astype(jnp.bfloat16)
        dims = (((1,), (axis,)), ((), ()))

        def dot(a, b):
            return lax.dot_general(a, b, dims, preferred_element_type=jnp.float32)

        return dot(high, high_ref[r]) + (dot(low, high_ref[r]) + dot(high, low_ref[r]))

    for r in range(rows):
        dir_ref[r] = res_ref[r] / theta
        inc_ref[r] = dir_ref[r]
    for step in range(ITERS):
        for r in range(rows):
            direction = dir_ref[r]
            middle = product(direction, r, 0) * inverse_var[r]
            residue = res_ref[r] - (product(middle, r, 1) + inverse_obs[r] * direction)
            direction = keep[step] * direction + gain[step] * residue
            res_ref[r] = residue
            dir_ref[r] = direction
            inc_ref[r] = inc_ref[r] + direction
    for r in range(rows):
        own = pltpu.roll(inc_ref[r], SPAN - HALO, 1)[:, :blocks]
        out_ref[pl.ds(r, blocks, stride=4), :] = own.T


def vmem(count):
    return [pl.BlockSpec(memory_space=pltpu.VMEM)] * count


def run_main(bounds, own, before, after):
    members, per_device = own.shape[1], 4
    blocks = own.shape[0] // CHUNK * 2
    return pl.pallas_call(
        main_kernel,
        out_shape=jax.ShapeDtypeStruct((blocks * per_device, members), jnp.float32),
        in_specs=[pl.BlockSpec(memory_space=pltpu.SMEM)] + vmem(3),
        out_specs=vmem(1)[0],
        scratch_shapes=[pltpu.VMEM((8 * SPAN, members), jnp.float32)]
        + [pltpu.VMEM((per_device, members, SPAN), jnp.float32)] * 4
        + [
            pltpu.VMEM((per_device, SPAN, SPAN), jnp.float32),
            pltpu.VMEM((per_device, SPAN, SPAN), jnp.bfloat16),
            pltpu.VMEM((per_device, SPAN, SPAN), jnp.bfloat16),
            pltpu.VMEM((REACH + 1, 8, LANES), jnp.float32),
            pltpu.VMEM((REACH, 8, LANES), jnp.float32),
            pltpu.VMEM((META, SPAN), jnp.float32),
        ],
        compiler_params=PARAMS,
        name="solve",
    )(bounds, own, before, after)


def on_device(ensemble, observed, obs_var, ridge, pred_back, bounds):
    local_blocks, rows, members = ensemble.shape
    slots = pred_back.shape[1]
    region_blocks = lax.axis_size("blk") * local_blocks
    regions = lax.axis_size("region")
    per_device = rows // lax.axis_size("blk")
    assert (local_blocks, per_device, members, region_blocks) == (2, 4, LANES, LANES)
    groups = rows // 8
    peers = 2 * groups
    packed = pl.pallas_call(
        pack_kernel,
        out_shape=jax.ShapeDtypeStruct((peers * CHUNK, members), jnp.float32),
        in_specs=[pl.BlockSpec(memory_space=pltpu.SMEM)] * 2 + vmem(3),
        out_specs=vmem(1)[0],
        compiler_params=PARAMS,
        name="pack",
    )(pred_back, ridge, ensemble, observed, obs_var)
    own = lax.all_to_all(packed.reshape(peers, 1, CHUNK * members), "blk", 0, 0, tiled=True)
    own = own.reshape(peers * CHUNK, members)
    up = [(i, i + 1) for i in range(regions - 1)]
    edge = HALO // local_blocks * CHUNK
    before = lax.ppermute(own[own.shape[0] - edge :], "region", up)
    after = lax.ppermute(own[:edge], "region", [(b, a) for a, b in up])
    increment = run_main(bounds, own, before, after)
    increment = increment.reshape(2 * groups, local_blocks * per_device, members)
    increment = lax.all_to_all(increment, "blk", 0, 0, tiled=True)
    return pl.pallas_call(
        add_kernel,
        out_shape=jax.ShapeDtypeStruct(ensemble.shape, jnp.float32),
        in_specs=vmem(2),
        out_specs=vmem(1)[0],
        compiler_params=PARAMS,
        name="add",
    )(ensemble, increment.reshape(groups, 2, 8, members))


def solution(mesh):
    return jax.shard_map(
        on_device,
        mesh=mesh,
        in_specs=(
            P(AXES, None, None),
            P(AXES, None, None),
            P(AXES, None),
            P(AXES),
            P(AXES, None),
            P(),
        ),
        out_specs=P(AXES, None, None),
        check_vma=False,
    )
```

time: 746 us -> 76.5 us (0.10)
  the two profiles are of different devices: /device:TPU:136 before, /device:TPU:193 now
where the time goes in v1:
time: 76.5 us; the launch traced here: 76.1 us
  blocking collectives  48.6 us (64%)
  Pallas kernels  9.18 us (12%)
  waiting for transfers between devices  7.16 us (9%)
  starting transfers between devices  7.13 us (9%)
  local copies, waits for them, and re-layouts  3.97 us (5%)
    all_to_all x1, blocking collectives, on_device(): lax.all_to_all(packed.reshape(peers, 1, CHUNK * members), 'blk', 0, 0, ti...  29 us
    all_to_all x1, blocking collectives, on_device(): increment = lax.all_to_all(increment, 'blk', 0, 0, tiled=True)  19.7 us
    pallas_call x1, Pallas kernels, run_main(): pl.pallas_call(main_kernel, out_shape=jax.ShapeDtypeStruct((blocks * per_...  7.54 us
    ppermute x1, starting transfers between devices, on_device(): before = lax.ppermute(own[own.shape[0] - edge:], 'region', up)  5.21 us
    ppermute x1, waiting for transfers between devices, on_device(): after = lax.ppermute(own[:edge], 'region', [(b, a) for a, b in up])  5.02 us
    unnamed x14, local copies, waits for them, and re-layouts  3.93 us
    ppermute x1, waiting for transfers between devices, on_device(): before = lax.ppermute(own[own.shape[0] - edge:], 'region', up)  2.14 us
    ppermute x1, starting transfers between devices, on_device(): after = lax.ppermute(own[:edge], 'region', [(b, a) for a, b in up])  1.92 us
  transfers between devices with their start and end apart: 2, of which 2 were waited for; matrix products, arithmetic and copies ran while one was open for 0% of the time, Pallas kernels for 0%

profile of v1, /device:TPU:193, one launch (start us, length us, event | category | flops | bytes accessed | tf_op | source)
XLA Modules:
  0.0 76.1 jit_solution(17937117373036420724)
XLA Ops:
  0.0 0.0 copy-start
  0.0 0.9 %copy-done = f32[2,256,128]{2,1,0:T(8,128)S(1)} copy-done((f32[2,256,128]{2,1,0:T(8,128)S(1)}, f32[2,256,128]{2,1,0:T(8,128)}, u32[]{:S(2)}) %copy-start) | copy-done | bytes 262168
  1.0 0.0 copy-start.2
  1.0 0.9 %copy-done.2 = f32[2,256,128]{2,1,0:T(8,128)S(1)} copy-done((f32[2,256,128]{2,1,0:T(8,128)S(1)}, f32[2,256,128]{2,1,0:T(8,128)}, u32[]{:S(2)}) %copy-start.2) | copy-done | bytes 262168
  1.9 0.0 copy-start.3
  1.9 0.7 copy-done.3
  2.6 0.0 copy-start.4
  2.6 0.7 copy-done.4
  3.3 0.0 copy-start.5
  3.3 0.7 copy-done.5
  3.9 0.9 %pack.1 = f32[1088,128]{1,0:T(8,128)S(1)} custom-call(s32[2,12]{1,0:T(2,128)S(1)} %copy-done.4, f32[2]{0:T(128)S(1)} %copy-done.5, f32[2,256,128]{2,1,0:T(8,128)S(1)} %copy-done, f32[2,256,128]{2,1,0:T(8,128)S(1)} %copy-done.2, f32[2,256]{1,0:T(2,128)S(1)} %copy-done.3), custom_call_target="tpu_custom_call" | custom-call | tf_op jit(solution)/shard_map/pack/pallas_call | solution.py:271
  4.8 29.0 %all_to_all.10 = f32[64,1,2176]{2,1,0:T(1,128)S(1)} all-to-all(f32[64,1,2176]{2,1,0:T(1,128)S(1)} %bitcast.7), channel_id=1, replica_groups=mesh['region'=8,'blk'=64] {'blk'}, dimensions={0} | all-to-all | bytes 1114112 | tf_op jit(solution)/shard_map/all_to_all | solution.py:279
  33.8 5.2 %collective-permute-start = (f32[408,128]{1,0:T(8,128)S(1)}, f32[408,128]{1,0:T(8,128)S(1)}, u32[]{:S(2)}, u32[]{:S(2)}) collective-permute-start(f32[408,128]{1,0:T(8,128)S(1)} %bitcast.11), channel_id=1, source_target_pairs={{0,64},{64,128},{128,192},{192,256},{256,320},{320,384},{384,448},... | collective-permute-start | bytes 626696 | tf_op jit(solution)/shard_map/ppermute | solution.py:283
  39.1 0.0 copy-start.6
  39.1 1.9 %collective-permute-start.1 = (f32[408,128]{1,0:T(8,128)S(1)}, f32[408,128]{1,0:T(8,128)S(1)}, u32[]{:S(2)}, u32[]{:S(2)}) collective-permute-start(f32[408,128]{1,0:T(8,128)S(1)} %bitcast.10), channel_id=1, source_target_pairs={{64,0},{128,64},{192,128},{256,192},{320,256},{384,320},{448,384},... | collective-permute-start | bytes 626696 | tf_op jit(solution)/shard_map/ppermute | solution.py:284
  41.0 2.1 %collective-permute-done.before_ref = f32[408,128]{1,0:T(8,128)S(1)} collective-permute-done((f32[408,128]{1,0:T(8,128)S(1)}, f32[408,128]{1,0:T(8,128)S(1)}, u32[]{:S(2)}, u32[]{:S(2)}) %collective-permute-start) | collective-permute-done | bytes 208928 | tf_op jit(solution)/shard_map/ppermute | solution.py:283
  43.1 5.0 %collective-permute-done.1.after_ref = f32[408,128]{1,0:T(8,128)S(1)} collective-permute-done((f32[408,128]{1,0:T(8,128)S(1)}, f32[408,128]{1,0:T(8,128)S(1)}, u32[]{:S(2)}, u32[]{:S(2)}) %collective-permute-start.1) | collective-permute-done | bytes 208928 | tf_op jit(solution)/shard_map/ppermute | solution.py:284
  48.2 0.0 copy-done.6
  48.2 7.5 %solve.1 = f32[512,128]{1,0:T(8,128)S(1)} custom-call(f32[2]{0:T(128)S(1)} %copy-done.6, f32[1088,128]{1,0:T(8,128)S(1)} %bitcast.6, f32[408,128]{1,0:T(8,128)S(1)} %collective-permute-done.before_ref, f32[408,128]{1,0:T(8,128)S(1)} %collective-permute-done.1.after_ref), custom_call_target="tpu_custom_call" | custom-call | tf_op jit(solution)/shard_map/solve/pallas_call | solution.py:242
  55.7 0.0 copy-start.1
  55.7 19.7 %all_to_all.11 = f32[64,8,128]{2,1,0:T(8,128)S(1)} all-to-all(f32[64,8,128]{2,1,0:T(8,128)S(1)} %bitcast.9), channel_id=1, replica_groups=mesh['region'=8,'blk'=64] {'blk'}, dimensions={0} | all-to-all | bytes 524288 | tf_op jit(solution)/shard_map/all_to_all | solution.py:287
  75.4 0.0 copy-done.1
  75.4 0.7 add.1
  (1 shorter events, 0.0 us)
Async XLA Ops:
  0.0 0.9 %copy-start = (f32[2,256,128]{2,1,0:T(8,128)S(1)}, f32[2,256,128]{2,1,0:T(8,128)}, u32[]{:S(2)}) copy-start(f32[2,256,128]{2,1,0:T(8,128)} %ens_ref.3) | copy-start | bytes 786436
  1.0 0.9 %copy-start.2 = (f32[2,256,128]{2,1,0:T(8,128)S(1)}, f32[2,256,128]{2,1,0:T(8,128)}, u32[]{:S(2)}) copy-start(f32[2,256,128]{2,1,0:T(8,128)} %obs_ref.1) | copy-start | bytes 786436
  1.9 0.7 copy-start.3
  2.6 0.7 copy-start.4
  3.3 0.7 copy-start.5
  33.8 9.3 %collective-permute-start = (f32[408,128]{1,0:T(8,128)S(1)}, f32[408,128]{1,0:T(8,128)S(1)}, u32[]{:S(2)}, u32[]{:S(2)}) collective-permute-start(f32[408,128]{1,0:T(8,128)S(1)} %bitcast.11), channel_id=1, source_target_pairs={{0,64},{64,128},{128,192},{192,256},{256,320},{320,384},{384,448},... | collective-permute-start | bytes 626696 | tf_op jit(solution)/shard_map/ppermute | solution.py:283
  39.1 9.1 %copy-start.6 = (f32[2]{0:T(128)S(1)}, f32[2]{0:T(128)}, u32[]{:S(2)}) copy-start(f32[2]{0:T(128)} %bounds_ref.1) | copy-start | bytes 28
  39.1 9.1 %collective-permute-start.1 = (f32[408,128]{1,0:T(8,128)S(1)}, f32[408,128]{1,0:T(8,128)S(1)}, u32[]{:S(2)}, u32[]{:S(2)}) collective-permute-start(f32[408,128]{1,0:T(8,128)S(1)} %bitcast.10), channel_id=1, source_target_pairs={{64,0},{128,64},{192,128},{256,192},{320,256},{384,320},{448,384},... | collective-permute-start | bytes 626696 | tf_op jit(solution)/shard_map/ppermute | solution.py:284
  55.7 19.7 %copy-start.1 = (f32[2,256,128]{2,1,0:T(8,128)S(1)}, f32[2,256,128]{2,1,0:T(8,128)}, u32[]{:S(2)}) copy-start(f32[2,256,128]{2,1,0:T(8,128)} %ens_ref.3) | copy-start | bytes 786436

commit v2 on v1

--- a/solution.py
+++ b/solution.py
@@ -11,7 +11,9 @@
 AXES = ("region", "blk")
 LANES = 128
 SPAN = 256
-CHUNK = 17
+FIRST = 9
+SECOND = 8
+CHUNK = FIRST + SECOND
 META = 16
 HIGHEST = lax.Precision.HIGHEST
 PARAMS = pltpu.CompilerParams(vmem_limit_bytes=48 * 1024 * 1024)
@@ -21,7 +23,17 @@
     return lax.broadcasted_iota(jnp.int32, shape, axis)
 
 
-def pack_kernel(pred_ref, ridge_ref, ens_ref, obs_ref, var_ref, out_ref):
+def pack_kernel(
+    pred_hbm, ridge_hbm, ens_hbm, obs_hbm, var_hbm, out_ref,
+    pred_ref, ridge_ref, ens_ref, obs_ref, var_ref, sems,
+):
+    pairs = [
+        (ens_hbm, ens_ref), (var_hbm, var_ref), (pred_hbm, pred_ref), (ridge_hbm, ridge_ref),
+        (obs_hbm, obs_ref),
+    ]
+    copies = [pltpu.make_async_copy(a, b, sems.at[i]) for i, (a, b) in enumerate(pairs)]
+    for copy in copies:
+        copy.start()
     local_blocks, rows, members = ens_ref.shape
     slots = pred_ref.shape[1]
     last = members - 1
@@ -29,7 +41,20 @@
     low = iota((groups, 8, members), 1) < 4
     lane = iota((rows, members), 1)
     spot = iota((1, members), 1)
+
+    def deal(blocks, start):
+        blocks = [block.reshape(groups, 8, members) for block in blocks]
+        even = jnp.where(low, blocks[0], pltpu.roll(blocks[1], 4, 1))
+        odd = jnp.where(low, pltpu.roll(blocks[0], 4, 1), blocks[1])
+        for q in range(groups):
+            at = 2 * q * CHUNK + start
+            out_ref[at : at + 8, :] = even[q]
+            out_ref[at + CHUNK : at + CHUNK + 8, :] = odd[q]
+
+    for copy in copies[:4]:
+        copy.wait()
     meta = jnp.zeros((1, members), jnp.float32)
+    blocks = []
     for b in range(local_blocks):
         for k in range(slots):
             meta = jnp.where(spot == META * b + k, pred_ref[b, k].astype(jnp.float32), meta)
@@ -38,16 +63,12 @@
         anomaly = (ens - jnp.mean(ens, axis=1, keepdims=True)) * (1.0 / (members - 1) ** 0.5)
         folded = anomaly + anomaly[:, last:] * (1.0 / (members**0.5 - 1.0))
         variance = jnp.broadcast_to(var_ref[b : b + 1, :], (members, rows)).T
-        first = jnp.where(lane == last, variance, folded).reshape(groups, 8, members)
-        second = (obs_ref[b] - ens).reshape(groups, 8, members)
-        even = jnp.where(low, first, pltpu.roll(second, 4, 1))
-        odd = jnp.where(low, pltpu.roll(first, 4, 1), second)
-        for q in range(groups):
-            at = 2 * q * CHUNK + 8 * b
-            out_ref[at : at + 8, :] = even[q]
-            out_ref[at + CHUNK : at + CHUNK + 8, :] = odd[q]
+        blocks.append(jnp.where(lane == last, variance, folded))
+    deal(blocks, 0)
     for p in range(2 * groups):
-        out_ref[p * CHUNK + CHUNK - 1 : (p + 1) * CHUNK, :] = meta
+        out_ref[p * CHUNK + FIRST - 1 : p * CHUNK + FIRST, :] = meta
+    copies[4].wait()
+    deal([obs_ref[b] - ens_ref[b] for b in range(local_blocks)], FIRST)
 
 
 def add_kernel(ens_ref, inc_ref, out_ref):
@@ -87,28 +108,27 @@
     return beta
 
 
-def main_kernel(
-    bounds_ref, own_ref, before_ref, after_ref, out_ref,
-    tile_ref, x_ref, res_ref, dir_ref, inc_ref, exact_ref, high_ref, low_ref, sums_ref, beta_ref, meta_ref,
+def line_up(sources, tile_ref):
+    at = 0
+    for ref, stride, start in sources:
+        for s in range(start, ref.shape[0], stride):
+            tile_ref[at : at + 8, :] = ref[s : s + 8, :]
+            at += 8
+    tile_ref[at:, :] = jnp.zeros((tile_ref.shape[0] - at, tile_ref.shape[1]), jnp.float32)
+
+
+def regress_kernel(
+    own_ref, before_ref, after_ref, high_ref, low_ref, inverse_ref,
+    tile_ref, x_ref, exact_ref, sums_ref, beta_ref, meta_ref,
 ):
     rows = 4
     slots = 12
     members = LANES
-    sources = [before_ref, own_ref, after_ref]
-    counts = [ref.shape[0] // CHUNK for ref in sources]
-    blocks = 2 * counts[1]
-    chunks = sum(counts)
-    at = 0
-    for ref, count in zip(sources, counts):
-        for s in range(count):
-            tile_ref[at : at + 16, :] = ref[s * CHUNK : s * CHUNK + 16, :]
-            at += 16
-    tile_ref[at:, :] = jnp.zeros((tile_ref.shape[0] - at, members), jnp.float32)
-
-    def column(offset):
-        return tile_ref[pl.ds(offset, SPAN, stride=8), :].T
-
-    facts = [ref[pl.ds(CHUNK - 1, count, stride=CHUNK), :] for ref, count in zip(sources, counts)]
+    sources = [(before_ref, FIRST, 0), (own_ref, CHUNK, 0), (after_ref, FIRST, 0)]
+    line_up(sources, tile_ref)
+
+    facts = [ref[pl.ds(FIRST - 1, ref.shape[0] // n, stride=n), :] for ref, n, _ in sources]
+    chunks = sum(len(fact) for fact in facts)
     facts = jnp.concatenate(facts + [jnp.zeros((LANES - chunks, members), jnp.float32)], axis=0).T
     spread = iota((LANES, SPAN), 1) - 2 * iota((LANES, SPAN), 0)
     meta_ref[...] = sum(
@@ -121,28 +141,13 @@
         for b in range(2)
     )
 
-    lower = jnp.full((1, SPAN), bounds_ref[0], jnp.float32)
-    higher = jnp.full((1, SPAN), bounds_ref[1], jnp.float32)
-    theta = (higher + lower) / 2
-    delta = (higher - lower) / 2
-    sigma = theta / delta
-    rho = 1.0 / sigma
-    keep, gain = [], []
-    for _ in range(ITERS):
-        rho_next = 1.0 / (2 * sigma - rho)
-        keep.append(rho_next * rho)
-        gain.append(2 * rho_next / delta)
-        rho = rho_next
-
     member = iota((members, SPAN), 0)
-    inverse_obs = []
     for r in range(rows):
-        x = column(r)
+        x = tile_ref[pl.ds(r, SPAN, stride=4), :].T
         variance = x[members - 1 :, :]
-        inverse_obs.append(1.0 / jnp.where(variance > 0, variance, 1.0))
+        inverse_ref[4 + r : 5 + r, :] = 1.0 / jnp.where(variance > 0, variance, 1.0)
         x = jnp.where(member == members - 1, 0.0, x)
         x_ref[r] = x
-        res_ref[r] = column(4 + r) * inverse_obs[r]
         for lag in range(REACH + 1):
             other = pltpu.roll(x, lag, 1) if lag else x
             total = jnp.sum(x * other, axis=0, keepdims=True)
@@ -198,12 +203,31 @@
             high_ref[r, rest, lanes] = jnp.zeros(empty, jnp.bfloat16)
             low_ref[r, rest, lanes] = jnp.zeros(empty, jnp.bfloat16)
 
-    inverse_var = []
     for r in range(rows):
         resid = jnp.dot(
             x_ref[r], exact_ref[r], precision=HIGHEST, preferred_element_type=jnp.float32
         )
-        inverse_var.append(1.0 / (jnp.sum(resid * resid, axis=0, keepdims=True) + 1e-05))
+        total = jnp.sum(resid * resid, axis=0, keepdims=True)
+        inverse_ref[r : r + 1, :] = 1.0 / (total + 1e-05)
+
+
+def iterate_kernel(
+    bounds_hbm, own_ref, before_ref, after_ref, high_ref, low_ref, inverse_ref, out_ref,
+    tile_ref, res_ref, dir_ref, inc_ref, bounds_ref, sem,
+):
+    rows = 4
+    members = LANES
+    blocks = out_ref.shape[0] // rows
+    copy = pltpu.make_async_copy(bounds_hbm, bounds_ref, sem)
+    copy.start()
+    line_up([(before_ref, SECOND, 0), (own_ref, CHUNK, FIRST), (after_ref, SECOND, 0)], tile_ref)
+    copy.wait()
+    lower = jnp.full((1, SPAN), bounds_ref[0], jnp.float32)
+    higher = jnp.full((1, SPAN), bounds_ref[1], jnp.float32)
+    theta = (higher + lower) / 2
+    delta = (higher - lower) / 2
+    sigma = theta / delta
+    rho = 1.0 / sigma
 
     def product(value, r, axis):
         high = value.astype(jnp.bfloat16)
@@ -213,50 +237,102 @@
         def dot(a, b):
             return lax.dot_general(a, b, dims, preferred_element_type=jnp.float32)
 
-        return dot(high, high_ref[r]) + (dot(low, high_ref[r]) + dot(high, low_ref[r]))
+        both = dot(jnp.concatenate([high, low], axis=0), high_ref[r])
+        return both[:members] + (both[members:] + dot(high, low_ref[r]))
 
     for r in range(rows):
-        dir_ref[r] = res_ref[r] / theta
+        residue = tile_ref[pl.ds(r, SPAN, stride=rows), :].T * inverse_ref[4 + r : 5 + r, :]
+        res_ref[r] = residue
+        dir_ref[r] = residue / theta
         inc_ref[r] = dir_ref[r]
-    for step in range(ITERS):
+    for _ in range(ITERS):
+        rho_next = 1.0 / (2 * sigma - rho)
         for r in range(rows):
             direction = dir_ref[r]
-            middle = product(direction, r, 0) * inverse_var[r]
-            residue = res_ref[r] - (product(middle, r, 1) + inverse_obs[r] * direction)
-            direction = keep[step] * direction + gain[step] * residue
+            middle = product(direction, r, 0) * inverse_ref[r : r + 1, :]
+            applied = product(middle, r, 1) + inverse_ref[4 + r : 5 + r, :] * direction
+            residue = res_ref[r] - applied
+            direction = (rho_next * rho) * direction + (2 * rho_next / delta) * residue
             res_ref[r] = residue
             dir_ref[r] = direction
             inc_ref[r] = inc_ref[r] + direction
+        rho = rho_next
     for r in range(rows):
         own = pltpu.roll(inc_ref[r], SPAN - HALO, 1)[:, :blocks]
-        out_ref[pl.ds(r, blocks, stride=4), :] = own.T
+        out_ref[pl.ds(r, blocks, stride=rows), :] = own.T
 
 
 def vmem(count):
     return [pl.BlockSpec(memory_space=pltpu.VMEM)] * count
 
 
-def run_main(bounds, own, before, after):
-    members, per_device = own.shape[1], 4
-    blocks = own.shape[0] // CHUNK * 2
+def hbm(count):
+    return [pl.BlockSpec(memory_space=pltpu.HBM)] * count
+
+
+def pack(pred_back, ridge, ensemble, observed, obs_var):
+    local_blocks, rows, members = ensemble.shape
+    peers = rows // 4
+    operands = [
+        pltpu.with_memory_space_constraint(value, pltpu.HBM)
+        for value in (pred_back, ridge, ensemble, observed, obs_var)
+    ]
     return pl.pallas_call(
-        main_kernel,
-        out_shape=jax.ShapeDtypeStruct((blocks * per_device, members), jnp.float32),
-        in_specs=[pl.BlockSpec(memory_space=pltpu.SMEM)] + vmem(3),
+        pack_kernel,
+        out_shape=jax.ShapeDtypeStruct((peers * CHUNK, members), jnp.float32),
+        in_specs=hbm(5),
         out_specs=vmem(1)[0],
-        scratch_shapes=[pltpu.VMEM((8 * SPAN, members), jnp.float32)]
-        + [pltpu.VMEM((per_device, members, SPAN), jnp.float32)] * 4
-        + [
-            pltpu.VMEM((per_device, SPAN, SPAN), jnp.float32),
-            pltpu.VMEM((per_device, SPAN, SPAN), jnp.bfloat16),
-            pltpu.VMEM((per_device, SPAN, SPAN), jnp.bfloat16),
+        scratch_shapes=[
+            pltpu.SMEM(pred_back.shape, jnp.int32),
+            pltpu.SMEM(ridge.shape, jnp.float32),
+            pltpu.VMEM(ensemble.shape, jnp.float32),
+            pltpu.VMEM(observed.shape, jnp.float32),
+            pltpu.VMEM(obs_var.shape, jnp.float32),
+            pltpu.SemaphoreType.DMA((5,)),
+        ],
+        compiler_params=PARAMS,
+        name="pack",
+    )(*operands)
+
+
+def regress(own, before, after):
+    members, rows = own.shape[1], 4
+    square = (rows, SPAN, SPAN)
+    return pl.pallas_call(
+        regress_kernel,
+        out_shape=[
+            jax.ShapeDtypeStruct(square, jnp.bfloat16),
+            jax.ShapeDtypeStruct(square, jnp.bfloat16),
+            jax.ShapeDtypeStruct((8, SPAN), jnp.float32),
+        ],
+        in_specs=vmem(3),
+        out_specs=vmem(3),
+        scratch_shapes=[
+            pltpu.VMEM((4 * SPAN, members), jnp.float32),
+            pltpu.VMEM((rows, members, SPAN), jnp.float32),
+            pltpu.VMEM(square, jnp.float32),
             pltpu.VMEM((REACH + 1, 8, LANES), jnp.float32),
             pltpu.VMEM((REACH, 8, LANES), jnp.float32),
             pltpu.VMEM((META, SPAN), jnp.float32),
         ],
         compiler_params=PARAMS,
-        name="solve",
-    )(bounds, own, before, after)
+        name="regress",
+    )(own, before, after)
+
+
+def iterate(bounds, own, before, after, factors):
+    members, rows = own.shape[1], 4
+    return pl.pallas_call(
+        iterate_kernel,
+        out_shape=jax.ShapeDtypeStruct((own.shape[0] // CHUNK * 2 * rows, members), jnp.float32),
+        in_specs=hbm(1) + vmem(6),
+        out_specs=vmem(1)[0],
+        scratch_shapes=[pltpu.VMEM((4 * SPAN, members), jnp.float32)]
+        + [pltpu.VMEM((rows, members, SPAN), jnp.float32)] * 3
+        + [pltpu.SMEM(bounds.shape, jnp.float32), pltpu.SemaphoreType.DMA],
+        compiler_params=PARAMS,
+        name="iterate",
+    )(pltpu.with_memory_space_constraint(bounds, pltpu.HBM), own, before, after, *factors)
 
 
 def on_device(ensemble, observed, obs_var, ridge, pred_back, bounds):
@@ -268,21 +344,21 @@
     assert (local_blocks, per_device, members, region_blocks) == (2, 4, LANES, LANES)
     groups = rows // 8
     peers = 2 * groups
-    packed = pl.pallas_call(
-        pack_kernel,
-        out_shape=jax.ShapeDtypeStruct((peers * CHUNK, members), jnp.float32),
-        in_specs=[pl.BlockSpec(memory_space=pltpu.SMEM)] * 2 + vmem(3),
-        out_specs=vmem(1)[0],
-        compiler_params=PARAMS,
-        name="pack",
-    )(pred_back, ridge, ensemble, observed, obs_var)
+    up = [(i, i + 1) for i in range(regions - 1)]
+    down = [(b, a) for a, b in up]
+
+    packed = pack(pred_back, ridge, ensemble, observed, obs_var)
     own = lax.all_to_all(packed.reshape(peers, 1, CHUNK * members), "blk", 0, 0, tiled=True)
+    edge = HALO // local_blocks
+
+    def halo(start, rows):
+        part = own[:, :, start * members : (start + rows) * members]
+        pieces = [lax.ppermute(part[peers - edge :], "region", up), lax.ppermute(part[:edge], "region", down)]
+        return [piece.reshape(edge * rows, members) for piece in pieces]
+
+    first, second = halo(0, FIRST), halo(FIRST, SECOND)
     own = own.reshape(peers * CHUNK, members)
-    up = [(i, i + 1) for i in range(regions - 1)]
-    edge = HALO // local_blocks * CHUNK
-    before = lax.ppermute(own[own.shape[0] - edge :], "region", up)
-    after = lax.ppermute(own[:edge], "region", [(b, a) for a, b in up])
-    increment = run_main(bounds, own, before, after)
+    increment = iterate(bounds, own, *second, regress(own, *first))
     increment = increment.reshape(2 * groups, local_blocks * per_device, members)
     increment = lax.all_to_all(increment, "blk", 0, 0, tiled=True)
     return pl.pallas_call(

time: 76.5 us -> 72.4 us (0.946)
  waiting for transfers between devices: 7.16 us -> 0.01 us
  starting transfers between devices: 7.13 us -> 13.6 us
  local copies, waits for them, and re-layouts: 3.97 us -> 0.05 us
    ppermute x2 -> x4, waiting for transfers between devices: 7.16 us -> 0.01 us  [the longest x2 0.01 us: halo(): lax.ppermute(part[:edge], 'region', down)]
    ppermute x2 -> x4, starting transfers between devices: 7.13 us -> 13.6 us  [the longest x2 9.78 us: halo(): lax.ppermute(part[peers - edge:], 'region', up)]
    unnamed x14 -> x2, local copies, waits for them, and re-layouts: 3.93 us -> 0.01 us
    pallas_call x2 -> x3, Pallas kernels: 8.44 us -> 8.88 us  [the longest x1 4.21 us: regress(): pl.pallas_call(regress_kernel, out_shape=[jax.ShapeDtypeStruct(square, jn...]
  transfers between devices with their start and end apart: 2 -> 4, of which waited for: 2 -> 0; matrix products, arithmetic and copies ran while one was open for 0% -> 0% of each run, Pallas kernels for 0% -> 6%
where the time goes in v2:
time: 72.4 us; the launch traced here: 72.1 us
  blocking collectives  48.7 us (67%)
  starting transfers between devices  13.6 us (19%)
  Pallas kernels  9.62 us (13%)
    all_to_all x1, blocking collectives, on_device(): lax.all_to_all(packed.reshape(peers, 1, CHUNK * members), 'blk', 0, 0, ti...  29 us
    all_to_all x1, blocking collectives, on_device(): increment = lax.all_to_all(increment, 'blk', 0, 0, tiled=True)  19.7 us
    ppermute x2, starting transfers between devices, halo(): lax.ppermute(part[peers - edge:], 'region', up)  9.78 us
    pallas_call x1, Pallas kernels, regress(): pl.pallas_call(regress_kernel, out_shape=[jax.ShapeDtypeStruct(square, jn...  4.21 us
    ppermute x2, starting transfers between devices, halo(): lax.ppermute(part[:edge], 'region', down)  3.84 us
    pallas_call x1, Pallas kernels, iterate(): pl.pallas_call(iterate_kernel, out_shape=jax.ShapeDtypeStruct((own.shape[...  3.29 us
  transfers between devices with their start and end apart: 4, of which 0 were waited for; matrix products, arithmetic and copies ran while one was open for 0% of the time, Pallas kernels for 6%

profile of v2, /device:TPU:193, one launch (start us, length us, event | category | flops | bytes accessed | tf_op | source)
XLA Modules:
  0.0 72.1 jit_solution(3252677045935909845)
XLA Ops:
  0.0 1.4 %pack.1 = f32[1088,128]{1,0:T(8,128)S(1)} custom-call(s32[2,12]{1,0:T(2,128)} %pred_hbm.1, f32[2]{0:T(128)} %ridge_hbm.1, f32[2,256,128]{2,1,0:T(8,128)} %ens_ref.1, f32[2,256,128]{2,1,0:T(8,128)} %obs_hbm.1, f32[2,256]{1,0:T(2,128)} %var_hbm.1), custom_call_target="tpu_custom_call" | custom-call | tf_op jit(solution)/shard_map/pack/pallas_call | solution.py:280
  1.4 29.0 %all_to_all.10 = f32[64,1,2176]{2,1,0:T(1,128)S(1)} all-to-all(f32[64,1,2176]{2,1,0:T(1,128)S(1)} %bitcast.10), channel_id=1, replica_groups=mesh['region'=8,'blk'=64] {'blk'}, dimensions={0} | all-to-all | bytes 1114112 | tf_op jit(solution)/shard_map/all_to_all | solution.py:351
  30.4 1.9 %collective-permute-start.3 = (f32[24,1,1152]{2,1,0:T(1,128)S(1)}, f32[24,1,1152]{2,1,0:T(1,128)S(1)}, u32[]{:S(2)}, u32[]{:S(2)}) collective-permute-start(f32[24,1,1152]{2,1,0:T(1,128)S(1)} %get-tuple-element.11), channel_id=1, source_target_pairs={{64,0},{128,64},{192,128},{256,192},{320,256},{384,320},{448,384},... | collective-permute-start | bytes 331784 | tf_op jit(solution)/shard_map/ppermute | solution.py:356
  32.3 5.2 %collective-permute-start.2 = (f32[24,1,1152]{2,1,0:T(1,128)S(1)}, f32[24,1,1152]{2,1,0:T(1,128)S(1)}, u32[]{:S(2)}, u32[]{:S(2)}) collective-permute-start(f32[24,1,1152]{2,1,0:T(1,128)S(1)} %get-tuple-element.12), channel_id=1, source_target_pairs={{0,64},{64,128},{128,192},{192,256},{256,320},{320,384},{384,448},... | collective-permute-start | bytes 331784 | tf_op jit(solution)/shard_map/ppermute | solution.py:356
  37.6 1.9 %collective-permute-start.1 = (f32[24,1,1024]{2,1,0:T(1,128)S(1)}, f32[24,1,1024]{2,1,0:T(1,128)S(1)}, u32[]{:S(2)}, u32[]{:S(2)}) collective-permute-start(f32[24,1,1024]{2,1,0:T(1,128)S(1)} %get-tuple-element.13), channel_id=1, source_target_pairs={{64,0},{128,64},{192,128},{256,192},{320,256},{384,320},{448,384},... | collective-permute-start | bytes 294920 | tf_op jit(solution)/shard_map/ppermute | solution.py:356
  39.5 4.6 %collective-permute-start = (f32[24,1,1024]{2,1,0:T(1,128)S(1)}, f32[24,1,1024]{2,1,0:T(1,128)S(1)}, u32[]{:S(2)}, u32[]{:S(2)}) collective-permute-start(f32[24,1,1024]{2,1,0:T(1,128)S(1)} %get-tuple-element.14), channel_id=1, source_target_pairs={{0,64},{64,128},{128,192},{192,256},{256,320},{320,384},{384,448},... | collective-permute-start | bytes 294920 | tf_op jit(solution)/shard_map/ppermute | solution.py:356
  44.1 0.0 collective-permute-done.3
  44.1 0.0 collective-permute-done.2
  44.1 4.2 %regress.1 = (bf16[4,256,256]{2,1,0:T(8,128)(2,1)S(1)}, bf16[4,256,256]{2,1,0:T(8,128)(2,1)S(1)}, f32[8,256]{1,0:T(8,128)S(1)}) custom-call(f32[1088,128]{1,0:T(8,128)S(1)} %bitcast.8, f32[216,128]{1,0:T(8,128)S(1)} %bitcast.14, f32[216,128]{1,0:T(8,128)S(1)} %bitcast.13), custom_call_target="tpu_custom_call" | custom-call | tf_op jit(solution)/shard_map/regress/pallas_call | solution.py:301
  48.3 0.0 collective-permute-done.1
  48.3 0.0 collective-permute-done
  48.3 3.3 %iterate.1 = f32[512,128]{1,0:T(8,128)S(1)} custom-call(f32[2]{0:T(128)} %bounds_hbm.1, f32[1088,128]{1,0:T(8,128)S(1)} %bitcast.9, f32[192,128]{1,0:T(8,128)S(1)} %bitcast.16, f32[192,128]{1,0:T(8,128)S(1)} %bitcast.15, bf16[4,256,256]{2,1,0:T(8,128)(2,1)S(1)} %get-tuple-element.8.high_ref, bf16[4,256,256]{2,1,0:T(8,128)(2,1)S(1)} %get-tuple-element.9.low_ref, ...), custom_call_target="tpu_custom_call" | custom-call | tf_op jit(solution)/shard_map/iterate/pallas_call | solution.py:325
  51.6 0.0 copy-start
  51.6 19.7 %all_to_all.11 = f32[64,8,128]{2,1,0:T(8,128)S(1)} all-to-all(f32[64,8,128]{2,1,0:T(8,128)S(1)} %bitcast.11), channel_id=1, replica_groups=mesh['region'=8,'blk'=64] {'blk'}, dimensions={0} | all-to-all | bytes 524288 | tf_op jit(solution)/shard_map/all_to_all | solution.py:363
  71.3 0.0 copy-done
  71.3 0.7 %add.1 = f32[2,256,128]{2,1,0:T(8,128)} custom-call(f32[2,256,128]{2,1,0:T(8,128)S(1)} %copy-done, f32[32,2,8,128]{3,2,1,0:T(8,128)S(1)} %bitcast.12), custom_call_target="tpu_custom_call" | custom-call | tf_op jit(solution)/shard_map/add/pallas_call | solution.py:364
  (2 shorter events, 0.0 us)
Async XLA Ops:
  30.4 13.7 %collective-permute-start.3 = (f32[24,1,1152]{2,1,0:T(1,128)S(1)}, f32[24,1,1152]{2,1,0:T(1,128)S(1)}, u32[]{:S(2)}, u32[]{:S(2)}) collective-permute-start(f32[24,1,1152]{2,1,0:T(1,128)S(1)} %get-tuple-element.11), channel_id=1, source_target_pairs={{64,0},{128,64},{192,128},{256,192},{320,256},{384,320},{448,384},... | collective-permute-start | bytes 331784 | tf_op jit(solution)/shard_map/ppermute | solution.py:356
  32.3 11.8 %collective-permute-start.2 = (f32[24,1,1152]{2,1,0:T(1,128)S(1)}, f32[24,1,1152]{2,1,0:T(1,128)S(1)}, u32[]{:S(2)}, u32[]{:S(2)}) collective-permute-start(f32[24,1,1152]{2,1,0:T(1,128)S(1)} %get-tuple-element.12), channel_id=1, source_target_pairs={{0,64},{64,128},{128,192},{192,256},{256,320},{320,384},{384,448},... | collective-permute-start | bytes 331784 | tf_op jit(solution)/shard_map/ppermute | solution.py:356
  37.6 10.7 %collective-permute-start.1 = (f32[24,1,1024]{2,1,0:T(1,128)S(1)}, f32[24,1,1024]{2,1,0:T(1,128)S(1)}, u32[]{:S(2)}, u32[]{:S(2)}) collective-permute-start(f32[24,1,1024]{2,1,0:T(1,128)S(1)} %get-tuple-element.13), channel_id=1, source_target_pairs={{64,0},{128,64},{192,128},{256,192},{320,256},{384,320},{448,384},... | collective-permute-start | bytes 294920 | tf_op jit(solution)/shard_map/ppermute | solution.py:356
  39.5 8.8 %collective-permute-start = (f32[24,1,1024]{2,1,0:T(1,128)S(1)}, f32[24,1,1024]{2,1,0:T(1,128)S(1)}, u32[]{:S(2)}, u32[]{:S(2)}) collective-permute-start(f32[24,1,1024]{2,1,0:T(1,128)S(1)} %get-tuple-element.14), channel_id=1, source_target_pairs={{0,64},{64,128},{128,192},{192,256},{256,320},{320,384},{384,448},... | collective-permute-start | bytes 294920 | tf_op jit(solution)/shard_map/ppermute | solution.py:356
  51.6 19.7 %copy-start = (f32[2,256,128]{2,1,0:T(8,128)S(1)}, f32[2,256,128]{2,1,0:T(8,128)}, u32[]{:S(2)}) copy-start(f32[2,256,128]{2,1,0:T(8,128)} %ens_ref.1) | copy-start | bytes 786436

commit v3 on v2

--- a/solution.py
+++ b/solution.py
@@ -108,28 +108,56 @@
     return beta
 
 
-def line_up(sources, tile_ref):
-    at = 0
-    for ref, stride, start in sources:
-        for s in range(start, ref.shape[0], stride):
-            tile_ref[at : at + 8, :] = ref[s : s + 8, :]
-            at += 8
-    tile_ref[at:, :] = jnp.zeros((tile_ref.shape[0] - at, tile_ref.shape[1]), jnp.float32)
-
-
-def regress_kernel(
-    own_ref, before_ref, after_ref, high_ref, low_ref, inverse_ref,
-    tile_ref, x_ref, exact_ref, sums_ref, beta_ref, meta_ref,
+def parity():
+    return lax.axis_index("blk") % 2
+
+
+def solve_kernel(
+    bounds_hbm, own_ref, first_ref, second_ref, out_ref,
+    tile_ref, fact_ref, x_ref, exact_ref, high_ref, low_ref, inverse_ref,
+    sums_ref, beta_ref, meta_ref, res_ref, dir_ref, inc_ref, bounds_ref, sem,
+):
+    copy = pltpu.make_async_copy(bounds_hbm, bounds_ref, sem)
+    copy.start()
+    edge = first_ref.shape[0] // CHUNK
+    peers = own_ref.shape[0] // CHUNK
+
+    def line_up(ref, at):
+        count = ref.shape[0] // CHUNK
+        for s in range(count):
+            for part, start in enumerate((0, FIRST)):
+                row = s * CHUNK + start
+                tile_ref[part, 8 * (at + s) : 8 * (at + s + 1), :] = ref[row : row + 8, :]
+        fact_ref[at : at + count, :] = ref[pl.ds(FIRST - 1, count, stride=CHUNK), :]
+
+    end = 2 * edge + peers
+    tile_ref[:, 8 * end :, :] = jnp.zeros((2, tile_ref.shape[1] - 8 * end, LANES), jnp.float32)
+    fact_ref[end:, :] = jnp.zeros((LANES - end, LANES), jnp.float32)
+    line_up(own_ref, edge)
+    for turn in range(2):
+
+        @pl.when(parity() == turn)
+        def _():
+            line_up((first_ref, second_ref)[turn], 0)
+            line_up((second_ref, first_ref)[turn], edge + peers)
+
+    regress(
+        tile_ref.at[0], fact_ref, high_ref, low_ref, inverse_ref,
+        x_ref, exact_ref, sums_ref, beta_ref, meta_ref,
+    )
+    copy.wait()
+    iterate(
+        bounds_ref, tile_ref.at[1], high_ref, low_ref, inverse_ref, out_ref, res_ref, dir_ref, inc_ref
+    )
+
+
+def regress(
+    tile_ref, fact_ref, high_ref, low_ref, inverse_ref, x_ref, exact_ref, sums_ref, beta_ref, meta_ref
 ):
     rows = 4
     slots = 12
     members = LANES
-    sources = [(before_ref, FIRST, 0), (own_ref, CHUNK, 0), (after_ref, FIRST, 0)]
-    line_up(sources, tile_ref)
-
-    facts = [ref[pl.ds(FIRST - 1, ref.shape[0] // n, stride=n), :] for ref, n, _ in sources]
-    chunks = sum(len(fact) for fact in facts)
-    facts = jnp.concatenate(facts + [jnp.zeros((LANES - chunks, members), jnp.float32)], axis=0).T
+    facts = fact_ref[...].T
     spread = iota((LANES, SPAN), 1) - 2 * iota((LANES, SPAN), 0)
     meta_ref[...] = sum(
         jnp.dot(
@@ -211,17 +239,10 @@
         inverse_ref[r : r + 1, :] = 1.0 / (total + 1e-05)
 
 
-def iterate_kernel(
-    bounds_hbm, own_ref, before_ref, after_ref, high_ref, low_ref, inverse_ref, out_ref,
-    tile_ref, res_ref, dir_ref, inc_ref, bounds_ref, sem,
-):
+def iterate(bounds_ref, tile_ref, high_ref, low_ref, inverse_ref, out_ref, res_ref, dir_ref, inc_ref):
     rows = 4
     members = LANES
     blocks = out_ref.shape[0] // rows
-    copy = pltpu.make_async_copy(bounds_hbm, bounds_ref, sem)
-    copy.start()
-    line_up([(before_ref, SECOND, 0), (own_ref, CHUNK, FIRST), (after_ref, SECOND, 0)], tile_ref)
-    copy.wait()
     lower = jnp.full((1, SPAN), bounds_ref[0], jnp.float32)
     higher = jnp.full((1, SPAN), bounds_ref[1], jnp.float32)
     theta = (higher + lower) / 2
@@ -295,44 +316,35 @@
     )(*operands)
 
 
-def regress(own, before, after):
+def solve(bounds, own, first, second):
     members, rows = own.shape[1], 4
     square = (rows, SPAN, SPAN)
+    wide = pltpu.VMEM((rows, members, SPAN), jnp.float32)
     return pl.pallas_call(
-        regress_kernel,
-        out_shape=[
-            jax.ShapeDtypeStruct(square, jnp.bfloat16),
-            jax.ShapeDtypeStruct(square, jnp.bfloat16),
-            jax.ShapeDtypeStruct((8, SPAN), jnp.float32),
-        ],
-        in_specs=vmem(3),
-        out_specs=vmem(3),
+        solve_kernel,
+        out_shape=jax.ShapeDtypeStruct((own.shape[0] // CHUNK * 2 * rows, members), jnp.float32),
+        in_specs=hbm(1) + vmem(3),
+        out_specs=vmem(1)[0],
         scratch_shapes=[
-            pltpu.VMEM((4 * SPAN, members), jnp.float32),
-            pltpu.VMEM((rows, members, SPAN), jnp.float32),
+            pltpu.VMEM((2, rows * SPAN, members), jnp.float32),
+            pltpu.VMEM((LANES, members), jnp.float32),
+            wide,
             pltpu.VMEM(square, jnp.float32),
+            pltpu.VMEM(square, jnp.bfloat16),
+            pltpu.VMEM(square, jnp.bfloat16),
+            pltpu.VMEM((8, SPAN), jnp.float32),
             pltpu.VMEM((REACH + 1, 8, LANES), jnp.float32),
             pltpu.VMEM((REACH, 8, LANES), jnp.float32),
             pltpu.VMEM((META, SPAN), jnp.float32),
+            wide,
+            wide,
+            wide,
+            pltpu.SMEM(bounds.shape, jnp.float32),
+            pltpu.SemaphoreType.DMA,
         ],
         compiler_params=PARAMS,
-        name="regress",
-    )(own, before, after)
-
-
-def iterate(bounds, own, before, after, factors):
-    members, rows = own.shape[1], 4
-    return pl.pallas_call(
-        iterate_kernel,
-        out_shape=jax.ShapeDtypeStruct((own.shape[0] // CHUNK * 2 * rows, members), jnp.float32),
-        in_specs=hbm(1) + vmem(6),
-        out_specs=vmem(1)[0],
-        scratch_shapes=[pltpu.VMEM((4 * SPAN, members), jnp.float32)]
-        + [pltpu.VMEM((rows, members, SPAN), jnp.float32)] * 3
-        + [pltpu.SMEM(bounds.shape, jnp.float32), pltpu.SemaphoreType.DMA],
-        compiler_params=PARAMS,
-        name="iterate",
-    )(pltpu.with_memory_space_constraint(bounds, pltpu.HBM), own, before, after, *factors)
+        name="solve",
+    )(pltpu.with_memory_space_constraint(bounds, pltpu.HBM), own, first, second)
 
 
 def on_device(ensemble, observed, obs_var, ridge, pred_back, bounds):
@@ -344,21 +356,24 @@
     assert (local_blocks, per_device, members, region_blocks) == (2, 4, LANES, LANES)
     groups = rows // 8
     peers = 2 * groups
-    up = [(i, i + 1) for i in range(regions - 1)]
-    down = [(b, a) for a, b in up]
-
     packed = pack(pred_back, ridge, ensemble, observed, obs_var)
     own = lax.all_to_all(packed.reshape(peers, 1, CHUNK * members), "blk", 0, 0, tiled=True)
     edge = HALO // local_blocks
 
-    def halo(start, rows):
-        part = own[:, :, start * members : (start + rows) * members]
-        pieces = [lax.ppermute(part[peers - edge :], "region", up), lax.ppermute(part[:edge], "region", down)]
-        return [piece.reshape(edge * rows, members) for piece in pieces]
-
-    first, second = halo(0, FIRST), halo(FIRST, SECOND)
-    own = own.reshape(peers * CHUNK, members)
-    increment = iterate(bounds, own, *second, regress(own, *first))
+    odd = lax.axis_index("blk") % 2
+    halo = []
+    for turn in range(2):
+        pairs = []
+        for region in range(regions):
+            for place in range(peers):
+                target = region + (1 if place % 2 == turn else -1)
+                if 0 <= target < regions:
+                    pairs.append((region * peers + place, target * peers + place))
+        start = jnp.where(odd == turn, peers - edge, 0)
+        part = lax.dynamic_slice_in_dim(own, start, edge, 0)
+        part = lax.ppermute(part, AXES, pairs)
+        halo.append(part.reshape(edge * CHUNK, members))
+    increment = solve(bounds, own.reshape(peers * CHUNK, members), *halo)
     increment = increment.reshape(2 * groups, local_blocks * per_device, members)
     increment = lax.all_to_all(increment, "blk", 0, 0, tiled=True)
     return pl.pallas_call(

time: 72.4 us -> 70.3 us (0.971)
  blocking collectives: 48.7 us -> 18.2 us
  waiting for transfers between devices: 0.01 us -> 24.2 us
  starting transfers between devices: 13.6 us -> 17.9 us
    all_to_all x1 -> x0, blocking collectives: 29 us -> none  [on_device(): lax.all_to_all(packed.reshape(peers, 1, CHUNK * members), 'blk', 0, 0, ti...]
    all_to_all x0 -> x1, waiting for transfers between devices: none -> 18.4 us  [on_device(): lax.all_to_all(packed.reshape(peers, 1, CHUNK * members), 'blk', 0, 0, ti...]
    all_to_all x0 -> x1, starting transfers between devices: none -> 10.8 us  [on_device(): lax.all_to_all(packed.reshape(peers, 1, CHUNK * members), 'blk', 0, 0, ti...]
    ppermute x4 -> x2, starting transfers between devices: 13.6 us -> 7.13 us  [on_device(): part = lax.ppermute(part, AXES, pairs)]
    ppermute x4 -> x2, waiting for transfers between devices: 0.01 us -> 5.83 us  [on_device(): part = lax.ppermute(part, AXES, pairs)]
    all_to_all x1, blocking collectives: 19.7 us -> 18.2 us  [on_device(): increment = lax.all_to_all(increment, 'blk', 0, 0, tiled=True)]
    pallas_call x2 -> x1, Pallas kernels: 7.5 us -> 6.68 us  [solve(): pl.pallas_call(solve_kernel, out_shape=jax.ShapeDtypeStruct((own.shape[0]...]
    pallas_call x1, Pallas kernels: 1.39 us -> 2.19 us  [pack(): pl.pallas_call(pack_kernel, out_shape=jax.ShapeDtypeStruct((peers * CHUNK...]
  transfers between devices with their start and end apart: 4 -> 3, of which waited for: 0 -> 3; matrix products, arithmetic and copies ran while one was open for 0% -> 0% of each run, Pallas kernels for 6% -> 0%
where the time goes in v3:
time: 70.3 us; the launch traced here: 70.1 us
  waiting for transfers between devices  24.2 us (34%)
  blocking collectives  18.2 us (26%)
  starting transfers between devices  17.9 us (25%)
  Pallas kernels  9.61 us (14%)
    all_to_all x1, waiting for transfers between devices, on_device(): lax.all_to_all(packed.reshape(peers, 1, CHUNK * members), 'blk', 0, 0, ti...  18.4 us
    all_to_all x1, blocking collectives, on_device(): increment = lax.all_to_all(increment, 'blk', 0, 0, tiled=True)  18.2 us
    all_to_all x1, starting transfers between devices, on_device(): lax.all_to_all(packed.reshape(peers, 1, CHUNK * members), 'blk', 0, 0, ti...  10.8 us
    ppermute x2, starting transfers between devices, on_device(): part = lax.ppermute(part, AXES, pairs)  7.13 us
    pallas_call x1, Pallas kernels, solve(): pl.pallas_call(solve_kernel, out_shape=jax.ShapeDtypeStruct((own.shape[0]...  6.68 us
    ppermute x2, waiting for transfers between devices, on_device(): part = lax.ppermute(part, AXES, pairs)  5.83 us
    pallas_call x1, Pallas kernels, pack(): pl.pallas_call(pack_kernel, out_shape=jax.ShapeDtypeStruct((peers * CHUNK...  2.19 us
  transfers between devices with their start and end apart: 3, of which 3 were waited for; matrix products, arithmetic and copies ran while one was open for 0% of the time, Pallas kernels for 0%

profile of v3, /device:TPU:193, one launch (start us, length us, event | category | flops | bytes accessed | tf_op | source)
XLA Modules:
  0.0 70.1 jit_solution(10558174215638095194)
XLA Ops:
  0.0 2.2 %pack.1 = f32[1088,128]{1,0:T(8,128)} custom-call(s32[2,12]{1,0:T(2,128)} %pred_hbm.1, f32[2]{0:T(128)} %ridge_hbm.1, f32[2,256,128]{2,1,0:T(8,128)} %ens_ref.1, f32[2,256,128]{2,1,0:T(8,128)} %obs_hbm.1, f32[2,256]{1,0:T(2,128)} %var_hbm.1), custom_call_target="tpu_custom_call" | custom-call | tf_op jit(solution)/shard_map/pack/pallas_call | solution.py:301
  2.2 10.8 %all-to-all-start = ((f32[64,1,2176]{2,1,0:T(1,128)}), f32[64,1,2176]{2,1,0:T(1,128)S(1)}, u32[]{:S(2)}, u32[]{:S(2)}) async-start(f32[64,1,2176]{2,1,0:T(1,128)} %bitcast), calls=%async_computation | async-start | bytes 1114112 | tf_op jit(solution)/shard_map/all_to_all | solution.py:360
  13.0 18.4 %all-to-all-done = f32[64,1,2176]{2,1,0:T(1,128)S(1)} async-done(((f32[64,1,2176]{2,1,0:T(1,128)}), f32[64,1,2176]{2,1,0:T(1,128)S(1)}, u32[]{:S(2)}, u32[]{:S(2)}) %all-to-all-start) | async-done | bytes 557088 | tf_op jit(solution)/shard_map/all_to_all | solution.py:360
  31.4 0.1 constant_dynamic-slice_fusion
  31.5 5.2 %collective-permute-start.1 = (f32[24,1,2176]{2,1,0:T(1,128)S(1)}, f32[24,1,2176]{2,1,0:T(1,128)S(1)}, u32[]{:S(2)}, u32[]{:S(2)}) collective-permute-start(f32[24,1,2176]{2,1,0:T(1,128)S(1)} %get-tuple-element.5), channel_id=1, source_target_pairs={{1,65},{3,67},{5,69},{7,71},{9,73},{11,75},{13,77},{15,79},{17,81}... | collective-permute-start | bytes 626696 | tf_op jit(solution)/shard_map/ppermute | solution.py:374
  36.7 1.9 %collective-permute-start = (f32[24,1,2176]{2,1,0:T(1,128)S(1)}, f32[24,1,2176]{2,1,0:T(1,128)S(1)}, u32[]{:S(2)}, u32[]{:S(2)}) collective-permute-start(f32[24,1,2176]{2,1,0:T(1,128)S(1)} %get-tuple-element.6), channel_id=1, source_target_pairs={{0,64},{2,66},{4,68},{6,70},{8,72},{10,74},{12,76},{14,78},{16,80}... | collective-permute-start | bytes 626696 | tf_op jit(solution)/shard_map/ppermute | solution.py:374
  38.6 0.8 %collective-permute-done.1 = f32[24,1,2176]{2,1,0:T(1,128)S(1)} collective-permute-done((f32[24,1,2176]{2,1,0:T(1,128)S(1)}, f32[24,1,2176]{2,1,0:T(1,128)S(1)}, u32[]{:S(2)}, u32[]{:S(2)}) %collective-permute-start.1) | collective-permute-done | bytes 208928 | tf_op jit(solution)/shard_map/ppermute | solution.py:374
  39.4 5.0 %collective-permute-done = f32[24,1,2176]{2,1,0:T(1,128)S(1)} collective-permute-done((f32[24,1,2176]{2,1,0:T(1,128)S(1)}, f32[24,1,2176]{2,1,0:T(1,128)S(1)}, u32[]{:S(2)}, u32[]{:S(2)}) %collective-permute-start) | collective-permute-done | bytes 208928 | tf_op jit(solution)/shard_map/ppermute | solution.py:374
  44.4 6.7 %solve.1 = f32[512,128]{1,0:T(8,128)S(1)} custom-call(f32[2]{0:T(128)} %bounds_hbm.1, f32[1088,128]{1,0:T(8,128)S(1)} %bitcast.6, f32[408,128]{1,0:T(8,128)S(1)} %bitcast.10, f32[408,128]{1,0:T(8,128)S(1)} %bitcast.9), custom_call_target="tpu_custom_call" | custom-call | tf_op jit(solution)/shard_map/solve/pallas_call | solution.py:323
  51.1 0.0 copy-start
  51.1 18.2 %all_to_all.10 = f32[64,8,128]{2,1,0:T(8,128)S(1)} all-to-all(f32[64,8,128]{2,1,0:T(8,128)S(1)} %bitcast.8), channel_id=1, replica_groups=mesh['region'=8,'blk'=64] {'blk'}, dimensions={0} | all-to-all | bytes 524288 | tf_op jit(solution)/shard_map/all_to_all | solution.py:378
  69.3 0.0 copy-done
  69.3 0.7 %add.8 = f32[2,256,128]{2,1,0:T(8,128)} custom-call(f32[2,256,128]{2,1,0:T(8,128)S(1)} %copy-done, f32[32,2,8,128]{3,2,1,0:T(8,128)S(1)} %bitcast.7), custom_call_target="tpu_custom_call" | custom-call | tf_op jit(solution)/shard_map/add/pallas_call | solution.py:379
Async XLA Ops:
  2.2 29.2 %all-to-all-start = ((f32[64,1,2176]{2,1,0:T(1,128)}), f32[64,1,2176]{2,1,0:T(1,128)S(1)}, u32[]{:S(2)}, u32[]{:S(2)}) async-start(f32[64,1,2176]{2,1,0:T(1,128)} %bitcast), calls=%async_computation | async-start | bytes 1114112 | tf_op jit(solution)/shard_map/all_to_all | solution.py:360
  31.5 7.9 %collective-permute-start.1 = (f32[24,1,2176]{2,1,0:T(1,128)S(1)}, f32[24,1,2176]{2,1,0:T(1,128)S(1)}, u32[]{:S(2)}, u32[]{:S(2)}) collective-permute-start(f32[24,1,2176]{2,1,0:T(1,128)S(1)} %get-tuple-element.5), channel_id=1, source_target_pairs={{1,65},{3,67},{5,69},{7,71},{9,73},{11,75},{13,77},{15,79},{17,81}... | collective-permute-start | bytes 626696 | tf_op jit(solution)/shard_map/ppermute | solution.py:374
  36.7 7.8 %collective-permute-start = (f32[24,1,2176]{2,1,0:T(1,128)S(1)}, f32[24,1,2176]{2,1,0:T(1,128)S(1)}, u32[]{:S(2)}, u32[]{:S(2)}) collective-permute-start(f32[24,1,2176]{2,1,0:T(1,128)S(1)} %get-tuple-element.6), channel_id=1, source_target_pairs={{0,64},{2,66},{4,68},{6,70},{8,72},{10,74},{12,76},{14,78},{16,80}... | collective-permute-start | bytes 626696 | tf_op jit(solution)/shard_map/ppermute | solution.py:374
  51.1 18.2 %copy-start = (f32[2,256,128]{2,1,0:T(8,128)S(1)}, f32[2,256,128]{2,1,0:T(8,128)}, u32[]{:S(2)}) copy-start(f32[2,256,128]{2,1,0:T(8,128)} %ens_ref.1) | copy-start | bytes 786436

commit v4 on v3

--- a/solution.py
+++ b/solution.py
@@ -112,8 +112,43 @@
     return lax.axis_index("blk") % 2
 
 
+def lag_sums(x, sums_ref, row):
+    for lag in range(REACH + 1):
+        other = pltpu.roll(x, lag, 1) if lag else x
+        sums_ref[lag, row : row + 1, :] = jnp.sum(x * other, axis=0, keepdims=True)
+
+
+def line_up(ref, tile_ref, at, parts=(0, 1), first=0, count=None):
+    for s in range(first, first + (count or ref.shape[0] // CHUNK)):
+        for part in parts:
+            row = s * CHUNK + (0, FIRST)[part]
+            tile_ref[part, 8 * at : 8 * (at + 1), :] = ref[row : row + 8, :]
+        at += 1
+
+
+def columns(tile_ref, r, x_ref, res_ref, inverse_ref, lanes):
+    members = LANES
+    x = tile_ref[0, pl.ds(r, LANES, stride=4), :].T
+    variance = x[members - 1 :, :]
+    inverse = 1.0 / jnp.where(variance > 0, variance, 1.0)
+    x = jnp.where(iota((members, LANES), 0) == members - 1, 0.0, x)
+    x_ref[r, :, lanes] = x
+    res_ref[r, :, lanes] = tile_ref[1, pl.ds(r, LANES, stride=4), :].T * inverse
+    inverse_ref[4 + r : 5 + r, lanes] = inverse
+    return x
+
+
+def local_kernel(own_ref, x_ref, res_ref, inverse_ref, sums_ref, tile_ref):
+    line_up(own_ref, tile_ref, 0)
+    inverse_ref[0:4, :] = jnp.zeros((4, LANES), jnp.float32)
+    for r in range(4):
+        x = columns(tile_ref, r, x_ref, res_ref, inverse_ref, slice(0, LANES))
+        lag_sums(x, sums_ref, r)
+
+
 def solve_kernel(
-    bounds_hbm, own_ref, first_ref, second_ref, out_ref,
+    bounds_hbm, own_ref, first_ref, second_ref, own_x_ref, own_res_ref, own_inverse_ref, own_sums_ref,
+    out_ref,
     tile_ref, fact_ref, x_ref, exact_ref, high_ref, low_ref, inverse_ref,
     sums_ref, beta_ref, meta_ref, res_ref, dir_ref, inc_ref, bounds_ref, sem,
 ):
@@ -121,42 +156,44 @@
     copy.start()
     edge = first_ref.shape[0] // CHUNK
     peers = own_ref.shape[0] // CHUNK
-
-    def line_up(ref, at):
-        count = ref.shape[0] // CHUNK
-        for s in range(count):
-            for part, start in enumerate((0, FIRST)):
-                row = s * CHUNK + start
-                tile_ref[part, 8 * (at + s) : 8 * (at + s + 1), :] = ref[row : row + 8, :]
-        fact_ref[at : at + count, :] = ref[pl.ds(FIRST - 1, count, stride=CHUNK), :]
-
-    end = 2 * edge + peers
-    tile_ref[:, 8 * end :, :] = jnp.zeros((2, tile_ref.shape[1] - 8 * end, LANES), jnp.float32)
-    fact_ref[end:, :] = jnp.zeros((LANES - end, LANES), jnp.float32)
-    line_up(own_ref, edge)
+    reach = REACH // 2
+    after, before, head = reach, reach + edge, reach + 2 * edge
+
+    def facts(ref):
+        return ref[pl.ds(FIRST - 1, ref.shape[0] // CHUNK, stride=CHUNK), :]
+
+    own_facts = facts(own_ref)
+    fact_ref[0:peers, :] = own_facts
+    fact_ref[peers : peers + reach, :] = own_facts[peers - reach :]
+    fact_ref[peers + head :, :] = own_facts[:reach]
+    line_up(own_ref, tile_ref, 0, (0,), peers - reach, reach)
+    line_up(own_ref, tile_ref, head, (0,), 0, reach)
+    for at in (0, head):
+        tile_ref[1, 8 * at : 8 * (at + reach), :] = jnp.zeros((8 * reach, LANES), jnp.float32)
     for turn in range(2):
 
         @pl.when(parity() == turn)
         def _():
-            line_up((first_ref, second_ref)[turn], 0)
-            line_up((second_ref, first_ref)[turn], edge + peers)
-
-    regress(
-        tile_ref.at[0], fact_ref, high_ref, low_ref, inverse_ref,
-        x_ref, exact_ref, sums_ref, beta_ref, meta_ref,
-    )
+            for ref, at in (((first_ref, second_ref)[turn], before), ((second_ref, first_ref)[turn], after)):
+                line_up(ref, tile_ref, at)
+                fact_ref[peers + at : peers + at + edge, :] = facts(ref)
+
+    for r in range(4):
+        x_ref[r, :, :LANES] = own_x_ref[r]
+        res_ref[r, :, :LANES] = own_res_ref[r]
+    inverse_ref[:, :LANES] = own_inverse_ref[...]
+    for r in range(4):
+        x = columns(tile_ref, r, x_ref, res_ref, inverse_ref, slice(LANES, SPAN))
+        lag_sums(x, sums_ref, 4 + r)
+    sums_ref[:, 0:4, :] = own_sums_ref[...]
+    regress(fact_ref, high_ref, low_ref, inverse_ref, x_ref, exact_ref, sums_ref, beta_ref, meta_ref)
     copy.wait()
-    iterate(
-        bounds_ref, tile_ref.at[1], high_ref, low_ref, inverse_ref, out_ref, res_ref, dir_ref, inc_ref
-    )
-
-
-def regress(
-    tile_ref, fact_ref, high_ref, low_ref, inverse_ref, x_ref, exact_ref, sums_ref, beta_ref, meta_ref
-):
+    iterate(bounds_ref, high_ref, low_ref, inverse_ref, out_ref, res_ref, dir_ref, inc_ref)
+
+
+def regress(fact_ref, high_ref, low_ref, inverse_ref, x_ref, exact_ref, sums_ref, beta_ref, meta_ref):
     rows = 4
     slots = 12
-    members = LANES
     facts = fact_ref[...].T
     spread = iota((LANES, SPAN), 1) - 2 * iota((LANES, SPAN), 0)
     meta_ref[...] = sum(
@@ -169,28 +206,18 @@
         for b in range(2)
     )
 
-    member = iota((members, SPAN), 0)
-    for r in range(rows):
-        x = tile_ref[pl.ds(r, SPAN, stride=4), :].T
-        variance = x[members - 1 :, :]
-        inverse_ref[4 + r : 5 + r, :] = 1.0 / jnp.where(variance > 0, variance, 1.0)
-        x = jnp.where(member == members - 1, 0.0, x)
-        x_ref[r] = x
-        for lag in range(REACH + 1):
-            other = pltpu.roll(x, lag, 1) if lag else x
-            total = jnp.sum(x * other, axis=0, keepdims=True)
-            sums_ref[lag, r : r + 1, :] = total[:, :LANES]
-            sums_ref[lag, 4 + r : 5 + r, :] = total[:, LANES:]
-
     upper_half = iota((8, LANES), 0) >= 4
     lane = iota((8, LANES), 1)
 
     def packed(k):
         return jnp.where(upper_half, meta_ref[k : k + 1, LANES:], meta_ref[k : k + 1, :LANES])
 
-    def shifted(value, lag):
-        turned = pltpu.roll(value, lag, 1)
-        return jnp.where(lane < lag, pltpu.roll(turned, 4, 0), turned)
+    def crossed(value):
+        return pltpu.roll(pltpu.roll(value, REACH, 1), 4, 0)
+
+    edge_lane = lane < REACH
+    sums = [sums_ref[lag] for lag in range(REACH + 1)]
+    sums = [jnp.where(edge_lane, crossed(value), value) for value in sums]
 
     picks = [packed(k) for k in range(slots)]
     ridge = packed(slots)
@@ -203,33 +230,53 @@
     gram = {}
     for i in range(REACH):
         for j in range(i):
-            gram[i, j] = shifted(sums_ref[i - j], j + 1) * (used[i] * used[j])
-        gram[i, i] = jnp.where(used[i] > 0, shifted(sums_ref[0], i + 1) + ridge, 1.0)
-    target = [sums_ref[i + 1] * used[i] for i in range(REACH)]
+            gram[i, j] = pltpu.roll(sums[i - j], j + 1, 1) * (used[i] * used[j])
+        gram[i, i] = jnp.where(used[i] > 0, pltpu.roll(sums[0], i + 1, 1) + ridge, 1.0)
+    target = [sums[i + 1] * used[i] for i in range(REACH)]
     beta = solve_lags(gram, target)
+    known = (lane >= REACH) & (lane < REACH + HALO)
+    known = known | ((lane >= HALO + 2 * REACH) & (lane < REACH + 2 * HALO))
     for i in range(REACH):
-        beta_ref[i] = -beta[i]
-
-    for half in range(2):
-        start = 0 if half == 0 else LANES - REACH
-        stop = LANES * (half + 1)
-        shape = (stop - start, LANES)
-        lag_of = iota(shape, 1) + half * LANES - iota(shape, 0) - start
+        value = jnp.where(edge_lane & ~upper_half, crossed(beta[i]), beta[i])
+        beta_ref[i] = jnp.where(upper_half & ~known, 0.0, -value)
+
+    def fill(row, count, half, lag_of):
+        for at in range(row, row + count, 16):
+            part = lag_of[at - row : at - row + 16]
+            factors = [jnp.where(part == 0, 1.0, 0.0)] * rows
+            for lag in range(1, REACH + 1):
+                hit = part == lag
+                for r in range(rows):
+                    value = beta_ref[lag - 1, 4 * half + r : 4 * half + r + 1, :]
+                    factors[r] = jnp.where(hit, value, factors[r])
+            store(at, 16, half, factors)
+
+    def store(row, count, half, factors):
         lanes = slice(half * LANES, (half + 1) * LANES)
         for r in range(rows):
-            factor = jnp.where(lag_of == 0, 1.0, 0.0)
-            for lag in range(1, REACH + 1):
-                value = beta_ref[lag - 1, 4 * half + r : 4 * half + r + 1, :]
-                factor = jnp.where(lag_of == lag, value, factor)
-            high = factor.astype(jnp.bfloat16)
-            exact_ref[r, start:stop, lanes] = factor
-            high_ref[r, start:stop, lanes] = high
-            low_ref[r, start:stop, lanes] = (factor - high.astype(jnp.float32)).astype(jnp.bfloat16)
-            rest = slice(stop, SPAN) if half == 0 else slice(0, start)
-            empty = (rest.stop - rest.start, LANES)
-            exact_ref[r, rest, lanes] = jnp.zeros(empty, jnp.float32)
-            high_ref[r, rest, lanes] = jnp.zeros(empty, jnp.bfloat16)
-            low_ref[r, rest, lanes] = jnp.zeros(empty, jnp.bfloat16)
+            high = factors[r].astype(jnp.bfloat16)
+            low = (factors[r] - high.astype(jnp.float32)).astype(jnp.bfloat16)
+            exact_ref[r, row : row + count, lanes] = factors[r]
+            high_ref[r, row : row + count, lanes] = high
+            low_ref[r, row : row + count, lanes] = low
+
+    square = (LANES, LANES)
+    row, column = iota(square, 0), iota(square, 1)
+    lag_of = column - row
+    fill(0, LANES, 0, lag_of)
+    copied = (row < REACH) | (row >= LANES - REACH)
+    fill(LANES, LANES, 1, jnp.where(copied & (lag_of != 0), -1, lag_of))
+    corner = column[:REACH] - row[:REACH]
+    fill(LANES - REACH, REACH, 1, jnp.where(corner == 0, -1, corner))
+    before_end = REACH + 2 * HALO
+    corner = column[:REACH] - row[:REACH] + REACH
+    fill(LANES + before_end - REACH, REACH, 0, corner)
+    for start, stop, half in (
+        (0, LANES - REACH, 1),
+        (LANES, LANES + before_end - REACH, 0),
+        (LANES + before_end, SPAN, 0),
+    ):
+        store(start, stop - start, half, [jnp.zeros((stop - start, LANES), jnp.float32)] * rows)
 
     for r in range(rows):
         resid = jnp.dot(
@@ -239,7 +286,7 @@
         inverse_ref[r : r + 1, :] = 1.0 / (total + 1e-05)
 
 
-def iterate(bounds_ref, tile_ref, high_ref, low_ref, inverse_ref, out_ref, res_ref, dir_ref, inc_ref):
+def iterate(bounds_ref, high_ref, low_ref, inverse_ref, out_ref, res_ref, dir_ref, inc_ref):
     rows = 4
     members = LANES
     blocks = out_ref.shape[0] // rows
@@ -262,9 +309,7 @@
         return both[:members] + (both[members:] + dot(high, low_ref[r]))
 
     for r in range(rows):
-        residue = tile_ref[pl.ds(r, SPAN, stride=rows), :].T * inverse_ref[4 + r : 5 + r, :]
-        res_ref[r] = residue
-        dir_ref[r] = residue / theta
+        dir_ref[r] = res_ref[r] / theta
         inc_ref[r] = dir_ref[r]
     for _ in range(ITERS):
         rho_next = 1.0 / (2 * sigma - rho)
@@ -279,8 +324,7 @@
             inc_ref[r] = inc_ref[r] + direction
         rho = rho_next
     for r in range(rows):
-        own = pltpu.roll(inc_ref[r], SPAN - HALO, 1)[:, :blocks]
-        out_ref[pl.ds(r, blocks, stride=rows), :] = own.T
+        out_ref[pl.ds(r, blocks, stride=rows), :] = inc_ref[r, :, :blocks].T
 
 
 def vmem(count):
@@ -300,7 +344,7 @@
     ]
     return pl.pallas_call(
         pack_kernel,
-        out_shape=jax.ShapeDtypeStruct((peers * CHUNK, members), jnp.float32),
+        out_shape=pltpu.VMEM((peers * CHUNK, members), jnp.float32),
         in_specs=hbm(5),
         out_specs=vmem(1)[0],
         scratch_shapes=[
@@ -316,17 +360,36 @@
     )(*operands)
 
 
-def solve(bounds, own, first, second):
+def local(own):
+    members = own.shape[1]
+    flat = jax.ShapeDtypeStruct((4, members, LANES), jnp.float32)
+    return pl.pallas_call(
+        local_kernel,
+        out_shape=[
+            flat,
+            flat,
+            jax.ShapeDtypeStruct((8, LANES), jnp.float32),
+            jax.ShapeDtypeStruct((REACH + 1, 4, LANES), jnp.float32),
+        ],
+        in_specs=vmem(1),
+        out_specs=vmem(4),
+        scratch_shapes=[pltpu.VMEM((2, 4 * LANES, members), jnp.float32)],
+        compiler_params=PARAMS,
+        name="local",
+    )(own)
+
+
+def solve(bounds, own, first, second, mine):
     members, rows = own.shape[1], 4
     square = (rows, SPAN, SPAN)
     wide = pltpu.VMEM((rows, members, SPAN), jnp.float32)
     return pl.pallas_call(
         solve_kernel,
         out_shape=jax.ShapeDtypeStruct((own.shape[0] // CHUNK * 2 * rows, members), jnp.float32),
-        in_specs=hbm(1) + vmem(3),
+        in_specs=hbm(1) + vmem(7),
         out_specs=vmem(1)[0],
         scratch_shapes=[
-            pltpu.VMEM((2, rows * SPAN, members), jnp.float32),
+            pltpu.VMEM((2, rows * LANES, members), jnp.float32),
             pltpu.VMEM((LANES, members), jnp.float32),
             wide,
             pltpu.VMEM(square, jnp.float32),
@@ -344,7 +407,7 @@
         ],
         compiler_params=PARAMS,
         name="solve",
-    )(pltpu.with_memory_space_constraint(bounds, pltpu.HBM), own, first, second)
+    )(pltpu.with_memory_space_constraint(bounds, pltpu.HBM), own, first, second, *mine)
 
 
 def on_device(ensemble, observed, obs_var, ridge, pred_back, bounds):
@@ -373,7 +436,8 @@
         part = lax.dynamic_slice_in_dim(own, start, edge, 0)
         part = lax.ppermute(part, AXES, pairs)
         halo.append(part.reshape(edge * CHUNK, members))
-    increment = solve(bounds, own.reshape(peers * CHUNK, members), *halo)
+    own = own.reshape(peers * CHUNK, members)
+    increment = solve(bounds, own, *halo, local(own))
     increment = increment.reshape(2 * groups, local_blocks * per_device, members)
     increment = lax.all_to_all(increment, "blk", 0, 0, tiled=True)
     return pl.pallas_call(

time: 70.3 us -> 69.1 us (0.983)
  waiting for transfers between devices: 24.2 us -> 22.9 us
    pallas_call x1 -> x2, Pallas kernels: 2.19 us -> 3.53 us  [the longest x1 2.2 us: pack(): pl.pallas_call(pack_kernel, out_shape=pltpu.VMEM((peers * CHUNK, members)...]
    ppermute x2, waiting for transfers between devices: 5.83 us -> 4.49 us  [on_device(): part = lax.ppermute(part, AXES, pairs)]
    pallas_call x1, Pallas kernels: 6.68 us -> 5.43 us  [solve(): pl.pallas_call(solve_kernel, out_shape=jax.ShapeDtypeStruct((own.shape[0]...]
  transfers between devices with their start and end apart: 3 -> 3, of which waited for: 3 -> 2; matrix products, arithmetic and copies ran while one was open for 0% -> 0% of each run, Pallas kernels for 0% -> 2%
where the time goes in v4:
time: 69.1 us; the launch traced here: 68.8 us
  waiting for transfers between devices  22.9 us (33%)
  blocking collectives  18.2 us (26%)
  starting transfers between devices  17.9 us (26%)
  Pallas kernels  9.7 us (14%)
    all_to_all x1, waiting for transfers between devices, on_device(): lax.all_to_all(packed.reshape(peers, 1, CHUNK * members), 'blk', 0, 0, ti...  18.4 us
    all_to_all x1, blocking collectives, on_device(): increment = lax.all_to_all(increment, 'blk', 0, 0, tiled=True)  18.2 us
    all_to_all x1, starting transfers between devices, on_device(): lax.all_to_all(packed.reshape(peers, 1, CHUNK * members), 'blk', 0, 0, ti...  10.8 us
    ppermute x2, starting transfers between devices, on_device(): part = lax.ppermute(part, AXES, pairs)  7.13 us
    pallas_call x1, Pallas kernels, solve(): pl.pallas_call(solve_kernel, out_shape=jax.ShapeDtypeStruct((own.shape[0]...  5.43 us
    ppermute x2, waiting for transfers between devices, on_device(): part = lax.ppermute(part, AXES, pairs)  4.49 us
    pallas_call x1, Pallas kernels, pack(): pl.pallas_call(pack_kernel, out_shape=pltpu.VMEM((peers * CHUNK, members)...  2.2 us
  transfers between devices with their start and end apart: 3, of which 2 were waited for; matrix products, arithmetic and copies ran while one was open for 0% of the time, Pallas kernels for 2%

profile of v4, /device:TPU:193, one launch (start us, length us, event | category | flops | bytes accessed | tf_op | source)
XLA Modules:
  0.0 68.8 jit_solution(1484943177212974568)
XLA Ops:
  0.0 2.2 %pack.1 = f32[1088,128]{1,0:T(8,128)} custom-call(s32[2,12]{1,0:T(2,128)} %pred_hbm.1, f32[2]{0:T(128)} %ridge_hbm.1, f32[2,256,128]{2,1,0:T(8,128)} %ens_ref.1, f32[2,256,128]{2,1,0:T(8,128)} %obs_hbm.1, f32[2,256]{1,0:T(2,128)} %var_hbm.1), custom_call_target="tpu_custom_call" | custom-call | tf_op jit(solution)/shard_map/pack/pallas_call | solution.py:345
  2.2 10.8 %all-to-all-start = ((f32[64,1,2176]{2,1,0:T(1,128)}), f32[64,1,2176]{2,1,0:T(1,128)S(1)}, u32[]{:S(2)}, u32[]{:S(2)}) async-start(f32[64,1,2176]{2,1,0:T(1,128)} %bitcast), calls=%async_computation | async-start | bytes 1114112 | tf_op jit(solution)/shard_map/all_to_all | solution.py:423
  13.0 18.4 %all-to-all-done = f32[64,1,2176]{2,1,0:T(1,128)S(1)} async-done(((f32[64,1,2176]{2,1,0:T(1,128)}), f32[64,1,2176]{2,1,0:T(1,128)S(1)}, u32[]{:S(2)}, u32[]{:S(2)}) %all-to-all-start) | async-done | bytes 557088 | tf_op jit(solution)/shard_map/all_to_all | solution.py:423
  31.4 0.1 constant_dynamic-slice_fusion
  31.5 5.2 %collective-permute-start.1 = (f32[24,1,2176]{2,1,0:T(1,128)S(1)}, f32[24,1,2176]{2,1,0:T(1,128)S(1)}, u32[]{:S(2)}, u32[]{:S(2)}) collective-permute-start(f32[24,1,2176]{2,1,0:T(1,128)S(1)} %get-tuple-element.13), channel_id=1, source_target_pairs={{1,65},{3,67},{5,69},{7,71},{9,73},{11,75},{13,77},{15,79},{17,81}... | collective-permute-start | bytes 626696 | tf_op jit(solution)/shard_map/ppermute | solution.py:437
  36.7 1.9 %collective-permute-start = (f32[24,1,2176]{2,1,0:T(1,128)S(1)}, f32[24,1,2176]{2,1,0:T(1,128)S(1)}, u32[]{:S(2)}, u32[]{:S(2)}) collective-permute-start(f32[24,1,2176]{2,1,0:T(1,128)S(1)} %get-tuple-element.14), channel_id=1, source_target_pairs={{0,64},{2,66},{4,68},{6,70},{8,72},{10,74},{12,76},{14,78},{16,80}... | collective-permute-start | bytes 626696 | tf_op jit(solution)/shard_map/ppermute | solution.py:437
  38.6 1.3 %local.1 = (f32[4,128,128]{2,1,0:T(8,128)S(1)}, f32[4,128,128]{2,1,0:T(8,128)S(1)}, f32[8,128]{1,0:T(8,128)S(1)}, f32[17,4,128]{2,1,0:T(4,128)S(1)}) custom-call(f32[1088,128]{1,0:T(8,128)S(1)} %bitcast.6), custom_call_target="tpu_custom_call" | custom-call | tf_op jit(solution)/shard_map/local/pallas_call | solution.py:366
  39.9 0.0 collective-permute-done.1
  40.0 4.5 %collective-permute-done = f32[24,1,2176]{2,1,0:T(1,128)S(1)} collective-permute-done((f32[24,1,2176]{2,1,0:T(1,128)S(1)}, f32[24,1,2176]{2,1,0:T(1,128)S(1)}, u32[]{:S(2)}, u32[]{:S(2)}) %collective-permute-start) | collective-permute-done | bytes 208928 | tf_op jit(solution)/shard_map/ppermute | solution.py:437
  44.4 5.4 %solve.1 = f32[512,128]{1,0:T(8,128)S(1)} custom-call(f32[2]{0:T(128)} %bounds_hbm.1, f32[1088,128]{1,0:T(8,128)S(1)} %bitcast.7, f32[408,128]{1,0:T(8,128)S(1)} %bitcast.11, f32[408,128]{1,0:T(8,128)S(1)} %bitcast.10, f32[4,128,128]{2,1,0:T(8,128)S(1)} %get-tuple-element.9.own_x_ref, f32[4,128,128]{2,1,0:T(8,128)S(1)} %get-tuple-element.10.own_res_ref, ...), custom_call_target="tpu_custom_call" | custom-call | tf_op jit(solution)/shard_map/solve/pallas_call | solution.py:386
  49.9 0.0 copy-start
  49.9 18.2 %all_to_all.10 = f32[64,8,128]{2,1,0:T(8,128)S(1)} all-to-all(f32[64,8,128]{2,1,0:T(8,128)S(1)} %bitcast.8), channel_id=1, replica_groups=mesh['region'=8,'blk'=64] {'blk'}, dimensions={0} | all-to-all | bytes 524288 | tf_op jit(solution)/shard_map/all_to_all | solution.py:442
  68.1 0.0 copy-done
  68.1 0.7 %add.8 = f32[2,256,128]{2,1,0:T(8,128)} custom-call(f32[2,256,128]{2,1,0:T(8,128)S(1)} %copy-done, f32[32,2,8,128]{3,2,1,0:T(8,128)S(1)} %bitcast.9), custom_call_target="tpu_custom_call" | custom-call | tf_op jit(solution)/shard_map/add/pallas_call | solution.py:443
Async XLA Ops:
  2.2 29.2 %all-to-all-start = ((f32[64,1,2176]{2,1,0:T(1,128)}), f32[64,1,2176]{2,1,0:T(1,128)S(1)}, u32[]{:S(2)}, u32[]{:S(2)}) async-start(f32[64,1,2176]{2,1,0:T(1,128)} %bitcast), calls=%async_computation | async-start | bytes 1114112 | tf_op jit(solution)/shard_map/all_to_all | solution.py:423
  31.5 8.5 %collective-permute-start.1 = (f32[24,1,2176]{2,1,0:T(1,128)S(1)}, f32[24,1,2176]{2,1,0:T(1,128)S(1)}, u32[]{:S(2)}, u32[]{:S(2)}) collective-permute-start(f32[24,1,2176]{2,1,0:T(1,128)S(1)} %get-tuple-element.13), channel_id=1, source_target_pairs={{1,65},{3,67},{5,69},{7,71},{9,73},{11,75},{13,77},{15,79},{17,81}... | collective-permute-start | bytes 626696 | tf_op jit(solution)/shard_map/ppermute | solution.py:437
  36.7 7.8 %collective-permute-start = (f32[24,1,2176]{2,1,0:T(1,128)S(1)}, f32[24,1,2176]{2,1,0:T(1,128)S(1)}, u32[]{:S(2)}, u32[]{:S(2)}) collective-permute-start(f32[24,1,2176]{2,1,0:T(1,128)S(1)} %get-tuple-element.14), channel_id=1, source_target_pairs={{0,64},{2,66},{4,68},{6,70},{8,72},{10,74},{12,76},{14,78},{16,80}... | collective-permute-start | bytes 626696 | tf_op jit(solution)/shard_map/ppermute | solution.py:437
  49.9 18.2 %copy-start = (f32[2,256,128]{2,1,0:T(8,128)S(1)}, f32[2,256,128]{2,1,0:T(8,128)}, u32[]{:S(2)}) copy-start(f32[2,256,128]{2,1,0:T(8,128)} %ens_ref.1) | copy-start | bytes 786436

commit v5 on v4

--- a/solution.py
+++ b/solution.py
@@ -419,11 +419,14 @@
     assert (local_blocks, per_device, members, region_blocks) == (2, 4, LANES, LANES)
     groups = rows // 8
     peers = 2 * groups
+    odd = (lax.axis_index("blk") & 1).astype(jnp.uint32)
+    edge = HALO // local_blocks
+    starts = [(1 - odd) * (peers - edge), odd * (peers - edge)]
+    observed, *starts = lax.optimization_barrier((observed, *starts))
     packed = pack(pred_back, ridge, ensemble, observed, obs_var)
     own = lax.all_to_all(packed.reshape(peers, 1, CHUNK * members), "blk", 0, 0, tiled=True)
-    edge = HALO // local_blocks
-
-    odd = lax.axis_index("blk") % 2
+    flat = own.reshape(peers * CHUNK, members)
+    mine = local(flat)
     halo = []
     for turn in range(2):
         pairs = []
@@ -432,12 +435,13 @@
                 target = region + (1 if place % 2 == turn else -1)
                 if 0 <= target < regions:
                     pairs.append((region * peers + place, target * peers + place))
-        start = jnp.where(odd == turn, peers - edge, 0)
-        part = lax.dynamic_slice_in_dim(own, start, edge, 0)
+        none = jnp.uint32(0)
+        part = lax.dynamic_slice(own, (starts[turn], none, none), (edge, 1, own.shape[2]))
+        if turn == 1:
+            part, *mine = lax.optimization_barrier((part, *mine))
         part = lax.ppermute(part, AXES, pairs)
         halo.append(part.reshape(edge * CHUNK, members))
-    own = own.reshape(peers * CHUNK, members)
-    increment = solve(bounds, own, *halo, local(own))
+    increment = solve(bounds, flat, *halo, mine)
     increment = increment.reshape(2 * groups, local_blocks * per_device, members)
     increment = lax.all_to_all(increment, "blk", 0, 0, tiled=True)
     return pl.pallas_call(

time: 69.1 us -> 71.4 us (1.033)
  blocking collectives: 18.2 us -> 52.3 us
  waiting for transfers between devices: 22.9 us -> 2.72 us
  starting transfers between devices: 17.9 us -> 7.13 us
  Pallas kernels: 9.7 us -> 8.88 us
    all_to_all x0 -> x1, blocking collectives: none -> 29 us  [on_device(): lax.all_to_all(packed.reshape(peers, 1, CHUNK * members), 'blk', 0, 0, ti...]
    all_to_all x1 -> x0, waiting for transfers between devices: 18.4 us -> none  [on_device(): lax.all_to_all(packed.reshape(peers, 1, CHUNK * members), 'blk', 0, 0, ti...]
    all_to_all x1 -> x0, starting transfers between devices: 10.8 us -> none  [on_device(): lax.all_to_all(packed.reshape(peers, 1, CHUNK * members), 'blk', 0, 0, ti...]
    all_to_all x1, blocking collectives: 18.2 us -> 23.4 us  [on_device(): increment = lax.all_to_all(increment, 'blk', 0, 0, tiled=True)]
    ppermute x2, waiting for transfers between devices: 4.49 us -> 2.72 us  [on_device(): part = lax.ppermute(part, AXES, pairs)]
    pallas_call x1, Pallas kernels: 2.2 us -> 1.39 us  [pack(): pl.pallas_call(pack_kernel, out_shape=pltpu.VMEM((peers * CHUNK, members)...]
  transfers between devices with their start and end apart: 3 -> 2, of which waited for: 2 -> 1; matrix products, arithmetic and copies ran while one was open for 0% -> 0% of each run, Pallas kernels for 2% -> 2%
where the time goes in v5:
time: 71.4 us; the launch traced here: 71.2 us
  blocking collectives  52.3 us (73%)
  Pallas kernels  8.88 us (12%)
  starting transfers between devices  7.13 us (10%)
  waiting for transfers between devices  2.72 us (4%)
    all_to_all x1, blocking collectives, on_device(): lax.all_to_all(packed.reshape(peers, 1, CHUNK * members), 'blk', 0, 0, ti...  29 us
    all_to_all x1, blocking collectives, on_device(): increment = lax.all_to_all(increment, 'blk', 0, 0, tiled=True)  23.4 us
    ppermute x2, starting transfers between devices, on_device(): part = lax.ppermute(part, AXES, pairs)  7.13 us
    pallas_call x1, Pallas kernels, solve(): pl.pallas_call(solve_kernel, out_shape=jax.ShapeDtypeStruct((own.shape[0]...  5.43 us
    ppermute x2, waiting for transfers between devices, on_device(): part = lax.ppermute(part, AXES, pairs)  2.72 us
  transfers between devices with their start and end apart: 2, of which 1 were waited for; matrix products, arithmetic and copies ran while one was open for 0% of the time, Pallas kernels for 2%

profile of v5, /device:TPU:193, one launch (start us, length us, event | category | flops | bytes accessed | tf_op | source)
XLA Modules:
  0.0 71.2 jit_solution(9638174863129537529)
XLA Ops:
  0.0 1.4 %pack.1 = f32[1088,128]{1,0:T(8,128)S(1)} custom-call(s32[2,12]{1,0:T(2,128)} %pred_hbm.1, f32[2]{0:T(128)} %ridge_hbm.1, f32[2,256,128]{2,1,0:T(8,128)} %ens_ref.1, f32[2,256,128]{2,1,0:T(8,128)} %obs_hbm, f32[2,256]{1,0:T(2,128)} %var_hbm.1), custom_call_target="tpu_custom_call" | custom-call | tf_op jit(solution)/shard_map/pack/pallas_call | solution.py:345
  1.4 29.0 %all_to_all.10 = f32[64,1,2176]{2,1,0:T(1,128)S(1)} all-to-all(f32[64,1,2176]{2,1,0:T(1,128)S(1)} %bitcast.8), channel_id=1, replica_groups=mesh['region'=8,'blk'=64] {'blk'}, dimensions={0} | all-to-all | bytes 1114112 | tf_op jit(solution)/shard_map/all_to_all | solution.py:427
  30.4 0.1 constant_dynamic-slice_fusion
  30.4 1.9 %collective-permute-start = (f32[24,1,2176]{2,1,0:T(1,128)S(1)}, f32[24,1,2176]{2,1,0:T(1,128)S(1)}, u32[]{:S(2)}, u32[]{:S(2)}) collective-permute-start(f32[24,1,2176]{2,1,0:T(1,128)S(1)} %get-tuple-element.30), channel_id=1, source_target_pairs={{0,64},{2,66},{4,68},{6,70},{8,72},{10,74},{12,76},{14,78},{16,80}... | collective-permute-start | bytes 626696 | tf_op jit(solution)/shard_map/ppermute | solution.py:442
  32.4 1.3 %local.1 = (f32[4,128,128]{2,1,0:T(8,128)S(1)}, f32[4,128,128]{2,1,0:T(8,128)S(1)}, f32[8,128]{1,0:T(8,128)S(1)}, f32[17,4,128]{2,1,0:T(4,128)S(1)}) custom-call(f32[1088,128]{1,0:T(8,128)S(1)} %bitcast.6), custom_call_target="tpu_custom_call" | custom-call | tf_op jit(solution)/shard_map/local/pallas_call | solution.py:366
  33.7 5.2 %collective-permute-start.1 = (f32[24,1,2176]{2,1,0:T(1,128)S(1)}, f32[24,1,2176]{2,1,0:T(1,128)S(1)}, u32[]{:S(2)}, u32[]{:S(2)}) collective-permute-start(f32[24,1,2176]{2,1,0:T(1,128)S(1)} %get-tuple-element.24), channel_id=1, source_target_pairs={{1,65},{3,67},{5,69},{7,71},{9,73},{11,75},{13,77},{15,79},{17,81}... | collective-permute-start | bytes 626696 | tf_op jit(solution)/shard_map/ppermute | solution.py:442
  38.9 0.0 collective-permute-done
  38.9 2.7 %collective-permute-done.1 = f32[24,1,2176]{2,1,0:T(1,128)S(1)} collective-permute-done((f32[24,1,2176]{2,1,0:T(1,128)S(1)}, f32[24,1,2176]{2,1,0:T(1,128)S(1)}, u32[]{:S(2)}, u32[]{:S(2)}) %collective-permute-start.1) | collective-permute-done | bytes 208928 | tf_op jit(solution)/shard_map/ppermute | solution.py:442
  41.6 5.4 %solve.1 = f32[512,128]{1,0:T(8,128)S(1)} custom-call(f32[2]{0:T(128)} %bounds_hbm.1, f32[1088,128]{1,0:T(8,128)S(1)} %bitcast.7, f32[408,128]{1,0:T(8,128)S(1)} %bitcast.11, f32[408,128]{1,0:T(8,128)S(1)} %bitcast.12, f32[4,128,128]{2,1,0:T(8,128)S(1)} %get-tuple-element.25.own_x_ref, f32[4,128,128]{2,1,0:T(8,128)S(1)} %get-tuple-element.26.own_res_ref, ...), custom_call_target="tpu_custom_call" | custom-call | tf_op jit(solution)/shard_map/solve/pallas_call | solution.py:386
  47.1 0.0 copy-start
  47.1 23.4 %all_to_all.11 = f32[64,8,128]{2,1,0:T(8,128)S(1)} all-to-all(f32[64,8,128]{2,1,0:T(8,128)S(1)} %bitcast.9), channel_id=1, replica_groups=mesh['region'=8,'blk'=64] {'blk'}, dimensions={0} | all-to-all | bytes 524288 | tf_op jit(solution)/shard_map/all_to_all | solution.py:446
  70.4 0.0 copy-done
  70.4 0.7 %add.1 = f32[2,256,128]{2,1,0:T(8,128)} custom-call(f32[2,256,128]{2,1,0:T(8,128)S(1)} %copy-done, f32[32,2,8,128]{3,2,1,0:T(8,128)S(1)} %bitcast.10), custom_call_target="tpu_custom_call" | custom-call | tf_op jit(solution)/shard_map/add/pallas_call | solution.py:447
Async XLA Ops:
  30.4 8.5 %collective-permute-start = (f32[24,1,2176]{2,1,0:T(1,128)S(1)}, f32[24,1,2176]{2,1,0:T(1,128)S(1)}, u32[]{:S(2)}, u32[]{:S(2)}) collective-permute-start(f32[24,1,2176]{2,1,0:T(1,128)S(1)} %get-tuple-element.30), channel_id=1, source_target_pairs={{0,64},{2,66},{4,68},{6,70},{8,72},{10,74},{12,76},{14,78},{16,80}... | collective-permute-start | bytes 626696 | tf_op jit(solution)/shard_map/ppermute | solution.py:442
  33.7 7.9 %collective-permute-start.1 = (f32[24,1,2176]{2,1,0:T(1,128)S(1)}, f32[24,1,2176]{2,1,0:T(1,128)S(1)}, u32[]{:S(2)}, u32[]{:S(2)}) collective-permute-start(f32[24,1,2176]{2,1,0:T(1,128)S(1)} %get-tuple-element.24), channel_id=1, source_target_pairs={{1,65},{3,67},{5,69},{7,71},{9,73},{11,75},{13,77},{15,79},{17,81}... | collective-permute-start | bytes 626696 | tf_op jit(solution)/shard_map/ppermute | solution.py:442
  47.1 23.4 %copy-start = (f32[2,256,128]{2,1,0:T(8,128)S(1)}, f32[2,256,128]{2,1,0:T(8,128)}, u32[]{:S(2)}) copy-start(f32[2,256,128]{2,1,0:T(8,128)} %ens_ref.1) | copy-start | bytes 786436

commit v6 on v5

--- a/solution.py
+++ b/solution.py
@@ -437,8 +437,6 @@
                     pairs.append((region * peers + place, target * peers + place))
         none = jnp.uint32(0)
         part = lax.dynamic_slice(own, (starts[turn], none, none), (edge, 1, own.shape[2]))
-        if turn == 1:
-            part, *mine = lax.optimization_barrier((part, *mine))
         part = lax.ppermute(part, AXES, pairs)
         halo.append(part.reshape(edge * CHUNK, members))
     increment = solve(bounds, flat, *halo, mine)

time: 71.4 us -> 68 us (0.952)
  blocking collectives: 52.3 us -> 47.1 us
  waiting for transfers between devices: 2.72 us -> 4.49 us
    all_to_all x1, blocking collectives: 23.4 us -> 18.2 us  [on_device(): increment = lax.all_to_all(increment, 'blk', 0, 0, tiled=True)]
    ppermute x2, waiting for transfers between devices: 2.72 us -> 4.49 us  [on_device(): part = lax.ppermute(part, AXES, pairs)]
where the time goes in v6:
time: 68 us; the launch traced here: 67.8 us
  blocking collectives  47.1 us (69%)
  Pallas kernels  8.88 us (13%)
  starting transfers between devices  7.13 us (10%)
  waiting for transfers between devices  4.49 us (7%)
    all_to_all x1, blocking collectives, on_device(): lax.all_to_all(packed.reshape(peers, 1, CHUNK * members), 'blk', 0, 0, ti...  29 us
    all_to_all x1, blocking collectives, on_device(): increment = lax.all_to_all(increment, 'blk', 0, 0, tiled=True)  18.2 us
    ppermute x2, starting transfers between devices, on_device(): part = lax.ppermute(part, AXES, pairs)  7.13 us
    pallas_call x1, Pallas kernels, solve(): pl.pallas_call(solve_kernel, out_shape=jax.ShapeDtypeStruct((own.shape[0]...  5.43 us
    ppermute x2, waiting for transfers between devices, on_device(): part = lax.ppermute(part, AXES, pairs)  4.49 us
    pallas_call x1, Pallas kernels, pack(): pl.pallas_call(pack_kernel, out_shape=pltpu.VMEM((peers * CHUNK, members)...  1.39 us
  transfers between devices with their start and end apart: 2, of which 1 were waited for; matrix products, arithmetic and copies ran while one was open for 0% of the time, Pallas kernels for 2%

profile of v6, /device:TPU:193, one launch (start us, length us, event | category | flops | bytes accessed | tf_op | source)
XLA Modules:
  0.0 67.8 jit_solution(9561475551383853382)
XLA Ops:
  0.0 1.4 %pack.1 = f32[1088,128]{1,0:T(8,128)S(1)} custom-call(s32[2,12]{1,0:T(2,128)} %pred_hbm.1, f32[2]{0:T(128)} %ridge_hbm.1, f32[2,256,128]{2,1,0:T(8,128)} %ens_ref.1, f32[2,256,128]{2,1,0:T(8,128)} %obs_hbm, f32[2,256]{1,0:T(2,128)} %var_hbm.1), custom_call_target="tpu_custom_call" | custom-call | tf_op jit(solution)/shard_map/pack/pallas_call | solution.py:345
  1.4 29.0 %all_to_all.10 = f32[64,1,2176]{2,1,0:T(1,128)S(1)} all-to-all(f32[64,1,2176]{2,1,0:T(1,128)S(1)} %bitcast.8), channel_id=1, replica_groups=mesh['region'=8,'blk'=64] {'blk'}, dimensions={0} | all-to-all | bytes 1114112 | tf_op jit(solution)/shard_map/all_to_all | solution.py:427
  30.4 0.1 constant_dynamic-slice_fusion
  30.4 5.2 %collective-permute-start.1 = (f32[24,1,2176]{2,1,0:T(1,128)S(1)}, f32[24,1,2176]{2,1,0:T(1,128)S(1)}, u32[]{:S(2)}, u32[]{:S(2)}) collective-permute-start(f32[24,1,2176]{2,1,0:T(1,128)S(1)} %get-tuple-element.19), channel_id=1, source_target_pairs={{1,65},{3,67},{5,69},{7,71},{9,73},{11,75},{13,77},{15,79},{17,81}... | collective-permute-start | bytes 626696 | tf_op jit(solution)/shard_map/ppermute | solution.py:440
  35.6 1.9 %collective-permute-start = (f32[24,1,2176]{2,1,0:T(1,128)S(1)}, f32[24,1,2176]{2,1,0:T(1,128)S(1)}, u32[]{:S(2)}, u32[]{:S(2)}) collective-permute-start(f32[24,1,2176]{2,1,0:T(1,128)S(1)} %get-tuple-element.20), channel_id=1, source_target_pairs={{0,64},{2,66},{4,68},{6,70},{8,72},{10,74},{12,76},{14,78},{16,80}... | collective-permute-start | bytes 626696 | tf_op jit(solution)/shard_map/ppermute | solution.py:440
  37.6 1.3 %local.1 = (f32[4,128,128]{2,1,0:T(8,128)S(1)}, f32[4,128,128]{2,1,0:T(8,128)S(1)}, f32[8,128]{1,0:T(8,128)S(1)}, f32[17,4,128]{2,1,0:T(4,128)S(1)}) custom-call(f32[1088,128]{1,0:T(8,128)S(1)} %bitcast.6), custom_call_target="tpu_custom_call" | custom-call | tf_op jit(solution)/shard_map/local/pallas_call | solution.py:366
  38.9 0.0 collective-permute-done.1
  38.9 4.5 %collective-permute-done = f32[24,1,2176]{2,1,0:T(1,128)S(1)} collective-permute-done((f32[24,1,2176]{2,1,0:T(1,128)S(1)}, f32[24,1,2176]{2,1,0:T(1,128)S(1)}, u32[]{:S(2)}, u32[]{:S(2)}) %collective-permute-start) | collective-permute-done | bytes 208928 | tf_op jit(solution)/shard_map/ppermute | solution.py:440
  43.4 5.4 %solve.1 = f32[512,128]{1,0:T(8,128)S(1)} custom-call(f32[2]{0:T(128)} %bounds_hbm.1, f32[1088,128]{1,0:T(8,128)S(1)} %bitcast.7, f32[408,128]{1,0:T(8,128)S(1)} %bitcast.12, f32[408,128]{1,0:T(8,128)S(1)} %bitcast.11, f32[4,128,128]{2,1,0:T(8,128)S(1)} %get-tuple-element.15.own_x_ref, f32[4,128,128]{2,1,0:T(8,128)S(1)} %get-tuple-element.16.own_res_ref, ...), custom_call_target="tpu_custom_call" | custom-call | tf_op jit(solution)/shard_map/solve/pallas_call | solution.py:386
  48.8 0.0 copy-start
  48.9 18.2 %all_to_all.11 = f32[64,8,128]{2,1,0:T(8,128)S(1)} all-to-all(f32[64,8,128]{2,1,0:T(8,128)S(1)} %bitcast.9), channel_id=1, replica_groups=mesh['region'=8,'blk'=64] {'blk'}, dimensions={0} | all-to-all | bytes 524288 | tf_op jit(solution)/shard_map/all_to_all | solution.py:444
  67.0 0.0 copy-done
  67.0 0.7 %add.1 = f32[2,256,128]{2,1,0:T(8,128)} custom-call(f32[2,256,128]{2,1,0:T(8,128)S(1)} %copy-done, f32[32,2,8,128]{3,2,1,0:T(8,128)S(1)} %bitcast.10), custom_call_target="tpu_custom_call" | custom-call | tf_op jit(solution)/shard_map/add/pallas_call | solution.py:445
Async XLA Ops:
  30.4 8.5 %collective-permute-start.1 = (f32[24,1,2176]{2,1,0:T(1,128)S(1)}, f32[24,1,2176]{2,1,0:T(1,128)S(1)}, u32[]{:S(2)}, u32[]{:S(2)}) collective-permute-start(f32[24,1,2176]{2,1,0:T(1,128)S(1)} %get-tuple-element.19), channel_id=1, source_target_pairs={{1,65},{3,67},{5,69},{7,71},{9,73},{11,75},{13,77},{15,79},{17,81}... | collective-permute-start | bytes 626696 | tf_op jit(solution)/shard_map/ppermute | solution.py:440
  35.6 7.8 %collective-permute-start = (f32[24,1,2176]{2,1,0:T(1,128)S(1)}, f32[24,1,2176]{2,1,0:T(1,128)S(1)}, u32[]{:S(2)}, u32[]{:S(2)}) collective-permute-start(f32[24,1,2176]{2,1,0:T(1,128)S(1)} %get-tuple-element.20), channel_id=1, source_target_pairs={{0,64},{2,66},{4,68},{6,70},{8,72},{10,74},{12,76},{14,78},{16,80}... | collective-permute-start | bytes 626696 | tf_op jit(solution)/shard_map/ppermute | solution.py:440
  48.8 18.2 %copy-start = (f32[2,256,128]{2,1,0:T(8,128)S(1)}, f32[2,256,128]{2,1,0:T(8,128)}, u32[]{:S(2)}) copy-start(f32[2,256,128]{2,1,0:T(8,128)} %ens_ref.1) | copy-start | bytes 786436

commit v7 on v6

--- a/solution.py
+++ b/solution.py
@@ -109,7 +109,7 @@
 
 
 def parity():
-    return lax.axis_index("blk") % 2
+    return (lax.axis_index("blk") + lax.axis_index("region")) & 1
 
 
 def lag_sums(x, sums_ref, row):
@@ -174,7 +174,7 @@
 
         @pl.when(parity() == turn)
         def _():
-            for ref, at in (((first_ref, second_ref)[turn], before), ((second_ref, first_ref)[turn], after)):
+            for ref, at in (((first_ref, second_ref)[turn], after), ((second_ref, first_ref)[turn], before)):
                 line_up(ref, tile_ref, at)
                 fact_ref[peers + at : peers + at + edge, :] = facts(ref)
 
@@ -419,7 +419,7 @@
     assert (local_blocks, per_device, members, region_blocks) == (2, 4, LANES, LANES)
     groups = rows // 8
     peers = 2 * groups
-    odd = (lax.axis_index("blk") & 1).astype(jnp.uint32)
+    odd = parity().astype(jnp.uint32)
     edge = HALO // local_blocks
     starts = [(1 - odd) * (peers - edge), odd * (peers - edge)]
     observed, *starts = lax.optimization_barrier((observed, *starts))
@@ -432,7 +432,7 @@
         pairs = []
         for region in range(regions):
             for place in range(peers):
-                target = region + (1 if place % 2 == turn else -1)
+                target = region + (1 if (place + region) % 2 == turn else -1)
                 if 0 <= target < regions:
                     pairs.append((region * peers + place, target * peers + place))
         none = jnp.uint32(0)

time: 68 us -> 69.2 us (1.018)
  the two profiles are of different devices: /device:TPU:193 before, /device:TPU:129 now
where the time goes in v7:
time: 69.2 us; the launch traced here: 69 us
  blocking collectives  50.8 us (73%)
  Pallas kernels  8.88 us (13%)
  starting transfers between devices  5.91 us (9%)
  waiting for transfers between devices  3.29 us (5%)
    all_to_all x1, blocking collectives, on_device(): lax.all_to_all(packed.reshape(peers, 1, CHUNK * members), 'blk', 0, 0, ti...  29 us
    all_to_all x1, blocking collectives, on_device(): increment = lax.all_to_all(increment, 'blk', 0, 0, tiled=True)  21.8 us
    ppermute x2, starting transfers between devices, on_device(): part = lax.ppermute(part, AXES, pairs)  5.91 us
    pallas_call x1, Pallas kernels, solve(): pl.pallas_call(solve_kernel, out_shape=jax.ShapeDtypeStruct((own.shape[0]...  5.43 us
    ppermute x2, waiting for transfers between devices, on_device(): part = lax.ppermute(part, AXES, pairs)  3.29 us
    pallas_call x1, Pallas kernels, pack(): pl.pallas_call(pack_kernel, out_shape=pltpu.VMEM((peers * CHUNK, members)...  1.39 us
  transfers between devices with their start and end apart: 2, of which 2 were waited for; matrix products, arithmetic and copies ran while one was open for 0% of the time, Pallas kernels for 2%

profile of v7, /device:TPU:129, one launch (start us, length us, event | category | flops | bytes accessed | tf_op | source)
XLA Modules:
  0.0 69.0 jit_solution(17419999785813394)
XLA Ops:
  0.0 1.4 %pack.1 = f32[1088,128]{1,0:T(8,128)S(1)} custom-call(s32[2,12]{1,0:T(2,128)} %pred_hbm.1, f32[2]{0:T(128)} %ridge_hbm.1, f32[2,256,128]{2,1,0:T(8,128)} %ens_ref.1, f32[2,256,128]{2,1,0:T(8,128)} %obs_hbm, f32[2,256]{1,0:T(2,128)} %var_hbm.1), custom_call_target="tpu_custom_call" | custom-call | tf_op jit(solution)/shard_map/pack/pallas_call | solution.py:345
  1.4 29.0 %all_to_all.10 = f32[64,1,2176]{2,1,0:T(1,128)S(1)} all-to-all(f32[64,1,2176]{2,1,0:T(1,128)S(1)} %bitcast.8), channel_id=1, replica_groups=mesh['region'=8,'blk'=64] {'blk'}, dimensions={0} | all-to-all | bytes 1114112 | tf_op jit(solution)/shard_map/all_to_all | solution.py:427
  30.4 0.1 constant_dynamic-slice_fusion
  30.4 4.0 %collective-permute-start.1 = (f32[24,1,2176]{2,1,0:T(1,128)S(1)}, f32[24,1,2176]{2,1,0:T(1,128)S(1)}, u32[]{:S(2)}, u32[]{:S(2)}) collective-permute-start(f32[24,1,2176]{2,1,0:T(1,128)S(1)} %get-tuple-element.19), channel_id=1, source_target_pairs={{1,65},{3,67},{5,69},{7,71},{9,73},{11,75},{13,77},{15,79},{17,81}... | collective-permute-start | bytes 626696 | tf_op jit(solution)/shard_map/ppermute | solution.py:440
  34.4 1.9 %collective-permute-start = (f32[24,1,2176]{2,1,0:T(1,128)S(1)}, f32[24,1,2176]{2,1,0:T(1,128)S(1)}, u32[]{:S(2)}, u32[]{:S(2)}) collective-permute-start(f32[24,1,2176]{2,1,0:T(1,128)S(1)} %get-tuple-element.20), channel_id=1, source_target_pairs={{0,64},{2,66},{4,68},{6,70},{8,72},{10,74},{12,76},{14,78},{16,80}... | collective-permute-start | bytes 626696 | tf_op jit(solution)/shard_map/ppermute | solution.py:440
  36.4 1.3 %local.1 = (f32[4,128,128]{2,1,0:T(8,128)S(1)}, f32[4,128,128]{2,1,0:T(8,128)S(1)}, f32[8,128]{1,0:T(8,128)S(1)}, f32[17,4,128]{2,1,0:T(4,128)S(1)}) custom-call(f32[1088,128]{1,0:T(8,128)S(1)} %bitcast.6), custom_call_target="tpu_custom_call" | custom-call | tf_op jit(solution)/shard_map/local/pallas_call | solution.py:366
  37.7 0.2 collective-permute-done.1
  37.9 3.1 %collective-permute-done = f32[24,1,2176]{2,1,0:T(1,128)S(1)} collective-permute-done((f32[24,1,2176]{2,1,0:T(1,128)S(1)}, f32[24,1,2176]{2,1,0:T(1,128)S(1)}, u32[]{:S(2)}, u32[]{:S(2)}) %collective-permute-start) | collective-permute-done | bytes 208928 | tf_op jit(solution)/shard_map/ppermute | solution.py:440
  41.0 5.4 %solve.1 = f32[512,128]{1,0:T(8,128)S(1)} custom-call(f32[2]{0:T(128)} %bounds_hbm.1, f32[1088,128]{1,0:T(8,128)S(1)} %bitcast.7, f32[408,128]{1,0:T(8,128)S(1)} %bitcast.12, f32[408,128]{1,0:T(8,128)S(1)} %bitcast.11, f32[4,128,128]{2,1,0:T(8,128)S(1)} %get-tuple-element.15.own_x_ref, f32[4,128,128]{2,1,0:T(8,128)S(1)} %get-tuple-element.16.own_res_ref, ...), custom_call_target="tpu_custom_call" | custom-call | tf_op jit(solution)/shard_map/solve/pallas_call | solution.py:386
  46.4 0.0 copy-start
  46.4 21.8 %all_to_all.11 = f32[64,8,128]{2,1,0:T(8,128)S(1)} all-to-all(f32[64,8,128]{2,1,0:T(8,128)S(1)} %bitcast.9), channel_id=1, replica_groups=mesh['region'=8,'blk'=64] {'blk'}, dimensions={0} | all-to-all | bytes 524288 | tf_op jit(solution)/shard_map/all_to_all | solution.py:444
  68.3 0.0 copy-done
  68.3 0.7 %add.5 = f32[2,256,128]{2,1,0:T(8,128)} custom-call(f32[2,256,128]{2,1,0:T(8,128)S(1)} %copy-done, f32[32,2,8,128]{3,2,1,0:T(8,128)S(1)} %bitcast.10), custom_call_target="tpu_custom_call" | custom-call | tf_op jit(solution)/shard_map/add/pallas_call | solution.py:445
Async XLA Ops:
  30.4 7.5 %collective-permute-start.1 = (f32[24,1,2176]{2,1,0:T(1,128)S(1)}, f32[24,1,2176]{2,1,0:T(1,128)S(1)}, u32[]{:S(2)}, u32[]{:S(2)}) collective-permute-start(f32[24,1,2176]{2,1,0:T(1,128)S(1)} %get-tuple-element.19), channel_id=1, source_target_pairs={{1,65},{3,67},{5,69},{7,71},{9,73},{11,75},{13,77},{15,79},{17,81}... | collective-permute-start | bytes 626696 | tf_op jit(solution)/shard_map/ppermute | solution.py:440
  34.4 6.5 %collective-permute-start = (f32[24,1,2176]{2,1,0:T(1,128)S(1)}, f32[24,1,2176]{2,1,0:T(1,128)S(1)}, u32[]{:S(2)}, u32[]{:S(2)}) collective-permute-start(f32[24,1,2176]{2,1,0:T(1,128)S(1)} %get-tuple-element.20), channel_id=1, source_target_pairs={{0,64},{2,66},{4,68},{6,70},{8,72},{10,74},{12,76},{14,78},{16,80}... | collective-permute-start | bytes 626696 | tf_op jit(solution)/shard_map/ppermute | solution.py:440
  46.4 21.8 %copy-start = (f32[2,256,128]{2,1,0:T(8,128)S(1)}, f32[2,256,128]{2,1,0:T(8,128)}, u32[]{:S(2)}) copy-start(f32[2,256,128]{2,1,0:T(8,128)} %ens_ref.1) | copy-start | bytes 786436

commit v8 on v6

--- a/solution.py
+++ b/solution.py
@@ -147,13 +147,14 @@
 
 
 def solve_kernel(
-    bounds_hbm, own_ref, first_ref, second_ref, own_x_ref, own_res_ref, own_inverse_ref, own_sums_ref,
+    bounds_hbm, own_ref, third_ref, second_ref, first_ref, own_x_ref, own_res_ref, own_inverse_ref, own_sums_ref,
     out_ref,
     tile_ref, fact_ref, x_ref, exact_ref, high_ref, low_ref, inverse_ref,
     sums_ref, beta_ref, meta_ref, res_ref, dir_ref, inc_ref, bounds_ref, sem,
 ):
     copy = pltpu.make_async_copy(bounds_hbm, bounds_ref, sem)
     copy.start()
+    halo_refs = (first_ref, second_ref, third_ref)
     edge = first_ref.shape[0] // CHUNK
     peers = own_ref.shape[0] // CHUNK
     reach = REACH // 2
@@ -174,7 +175,7 @@
 
         @pl.when(parity() == turn)
         def _():
-            for ref, at in (((first_ref, second_ref)[turn], before), ((second_ref, first_ref)[turn], after)):
+            for ref, at in ((halo_refs[turn], after), (halo_refs[turn + 1], before)):
                 line_up(ref, tile_ref, at)
                 fact_ref[peers + at : peers + at + edge, :] = facts(ref)
 
@@ -379,14 +380,14 @@
     )(own)
 
 
-def solve(bounds, own, first, second, mine):
+def solve(bounds, own, halo, mine):
     members, rows = own.shape[1], 4
     square = (rows, SPAN, SPAN)
     wide = pltpu.VMEM((rows, members, SPAN), jnp.float32)
     return pl.pallas_call(
         solve_kernel,
         out_shape=jax.ShapeDtypeStruct((own.shape[0] // CHUNK * 2 * rows, members), jnp.float32),
-        in_specs=hbm(1) + vmem(7),
+        in_specs=hbm(1) + vmem(8),
         out_specs=vmem(1)[0],
         scratch_shapes=[
             pltpu.VMEM((2, rows * LANES, members), jnp.float32),
@@ -407,7 +408,7 @@
         ],
         compiler_params=PARAMS,
         name="solve",
-    )(pltpu.with_memory_space_constraint(bounds, pltpu.HBM), own, first, second, *mine)
+    )(pltpu.with_memory_space_constraint(bounds, pltpu.HBM), own, *halo[::-1], *mine)
 
 
 def on_device(ensemble, observed, obs_var, ridge, pred_back, bounds):
@@ -421,25 +422,28 @@
     peers = 2 * groups
     odd = (lax.axis_index("blk") & 1).astype(jnp.uint32)
     edge = HALO // local_blocks
-    starts = [(1 - odd) * (peers - edge), odd * (peers - edge)]
-    observed, *starts = lax.optimization_barrier((observed, *starts))
+    start = (1 - odd) * (peers - edge)
+    observed, start = lax.optimization_barrier((observed, start))
     packed = pack(pred_back, ridge, ensemble, observed, obs_var)
     own = lax.all_to_all(packed.reshape(peers, 1, CHUNK * members), "blk", 0, 0, tiled=True)
     flat = own.reshape(peers * CHUNK, members)
     mine = local(flat)
-    halo = []
-    for turn in range(2):
-        pairs = []
-        for region in range(regions):
-            for place in range(peers):
-                target = region + (1 if place % 2 == turn else -1)
-                if 0 <= target < regions:
-                    pairs.append((region * peers + place, target * peers + place))
-        none = jnp.uint32(0)
-        part = lax.dynamic_slice(own, (starts[turn], none, none), (edge, 1, own.shape[2]))
-        part = lax.ppermute(part, AXES, pairs)
-        halo.append(part.reshape(edge * CHUNK, members))
-    increment = solve(bounds, flat, *halo, mine)
+
+    def pairs(core, step):
+        return [
+            (region * peers + place, (region + step) * peers + place)
+            for region in range(regions)
+            for place in range(core, peers, 2)
+            if 0 <= region + step < regions
+        ]
+
+    none = jnp.uint32(0)
+    middle = lax.dynamic_slice(own, (start, none, none), (edge, 1, own.shape[2]))
+    first = lax.ppermute(own[:edge], AXES, pairs(0, -1))
+    second = lax.ppermute(middle, AXES, pairs(1, -1) + pairs(0, 1))
+    third = lax.ppermute(own[peers - edge :], AXES, pairs(1, 1))
+    halo = [part.reshape(edge * CHUNK, members) for part in (first, second, third)]
+    increment = solve(bounds, flat, halo, mine)
     increment = increment.reshape(2 * groups, local_blocks * per_device, members)
     increment = lax.all_to_all(increment, "blk", 0, 0, tiled=True)
     return pl.pallas_call(

time: 68 us -> 68.2 us (level)
  waiting for transfers between devices: 4.49 us -> 3.41 us
    ppermute x2 -> x3, waiting for transfers between devices: 4.49 us -> 3.41 us  [the longest x1 2.31 us: on_device(): second = lax.ppermute(middle, AXES, pairs(1, -1) + pairs(0, 1))]
    ppermute x2 -> x3, starting transfers between devices: 7.13 us -> 7.81 us  [the longest x1 5.21 us: on_device(): third = lax.ppermute(own[peers - edge:], AXES, pairs(1, 1))]
  transfers between devices with their start and end apart: 2 -> 3, of which waited for: 1 -> 2; matrix products, arithmetic and copies ran while one was open for 0% -> 0% of each run, Pallas kernels for 2% -> 2%
where the time goes in v8:
time: 68.2 us; the launch traced here: 67.9 us
  blocking collectives  47.7 us (70%)
  Pallas kernels  8.88 us (13%)
  starting transfers between devices  7.81 us (11%)
  waiting for transfers between devices  3.41 us (5%)
    all_to_all x1, blocking collectives, on_device(): lax.all_to_all(packed.reshape(peers, 1, CHUNK * members), 'blk', 0, 0, ti...  29 us
    all_to_all x1, blocking collectives, on_device(): increment = lax.all_to_all(increment, 'blk', 0, 0, tiled=True)  18.7 us
    pallas_call x1, Pallas kernels, solve(): pl.pallas_call(solve_kernel, out_shape=jax.ShapeDtypeStruct((own.shape[0]...  5.43 us
    ppermute x1, starting transfers between devices, on_device(): third = lax.ppermute(own[peers - edge:], AXES, pairs(1, 1))  5.21 us
    ppermute x1, waiting for transfers between devices, on_device(): second = lax.ppermute(middle, AXES, pairs(1, -1) + pairs(0, 1))  2.31 us
    ppermute x1, starting transfers between devices, on_device(): second = lax.ppermute(middle, AXES, pairs(1, -1) + pairs(0, 1))  1.92 us
    pallas_call x1, Pallas kernels, pack(): pl.pallas_call(pack_kernel, out_shape=pltpu.VMEM((peers * CHUNK, members)...  1.39 us
  transfers between devices with their start and end apart: 3, of which 2 were waited for; matrix products, arithmetic and copies ran while one was open for 0% of the time, Pallas kernels for 2%

profile of v8, /device:TPU:193, one launch (start us, length us, event | category | flops | bytes accessed | tf_op | source)
XLA Modules:
  0.0 67.9 jit_solution(14995970878058828484)
XLA Ops:
  0.0 1.4 %pack.1 = f32[1088,128]{1,0:T(8,128)S(1)} custom-call(s32[2,12]{1,0:T(2,128)} %pred_hbm.1, f32[2]{0:T(128)} %ridge_hbm.1, f32[2,256,128]{2,1,0:T(8,128)} %ens_ref.1, f32[2,256,128]{2,1,0:T(8,128)} %obs_hbm, f32[2,256]{1,0:T(2,128)} %var_hbm.1), custom_call_target="tpu_custom_call" | custom-call | tf_op jit(solution)/shard_map/pack/pallas_call | solution.py:346
  1.4 29.0 %all_to_all.10 = f32[64,1,2176]{2,1,0:T(1,128)S(1)} all-to-all(f32[64,1,2176]{2,1,0:T(1,128)S(1)} %bitcast.9), channel_id=1, replica_groups=mesh['region'=8,'blk'=64] {'blk'}, dimensions={0} | all-to-all | bytes 1114112 | tf_op jit(solution)/shard_map/all_to_all | solution.py:428
  30.4 0.1 fusion
  30.4 0.7 collective-permute-start.2
  31.1 1.9 %collective-permute-start.1 = (f32[24,1,2176]{2,1,0:T(1,128)S(1)}, f32[24,1,2176]{2,1,0:T(1,128)S(1)}, u32[]{:S(2)}, u32[]{:S(2)}) collective-permute-start(f32[24,1,2176]{2,1,0:T(1,128)S(1)} %get-tuple-element.18), channel_id=1, source_target_pairs={{65,1},{67,3},{69,5},{71,7},{73,9},{75,11},{77,13},{79,15},{81,17}... | collective-permute-start | bytes 626696 | tf_op jit(solution)/shard_map/ppermute | solution.py:443
  33.1 5.2 %collective-permute-start = (f32[24,1,2176]{2,1,0:T(1,128)S(1)}, f32[24,1,2176]{2,1,0:T(1,128)S(1)}, u32[]{:S(2)}, u32[]{:S(2)}) collective-permute-start(f32[24,1,2176]{2,1,0:T(1,128)S(1)} %get-tuple-element.19), channel_id=1, source_target_pairs={{1,65},{3,67},{5,69},{7,71},{9,73},{11,75},{13,77},{15,79},{17,81}... | collective-permute-start | bytes 626696 | tf_op jit(solution)/shard_map/ppermute | solution.py:444
  38.3 1.3 %local.1 = (f32[4,128,128]{2,1,0:T(8,128)S(1)}, f32[4,128,128]{2,1,0:T(8,128)S(1)}, f32[8,128]{1,0:T(8,128)S(1)}, f32[17,4,128]{2,1,0:T(4,128)S(1)}) custom-call(f32[1088,128]{1,0:T(8,128)S(1)} %bitcast.7), custom_call_target="tpu_custom_call" | custom-call | tf_op jit(solution)/shard_map/local/pallas_call | solution.py:367
  39.6 0.0 collective-permute-done.2
  39.6 2.3 %collective-permute-done.1 = f32[24,1,2176]{2,1,0:T(1,128)S(1)} collective-permute-done((f32[24,1,2176]{2,1,0:T(1,128)S(1)}, f32[24,1,2176]{2,1,0:T(1,128)S(1)}, u32[]{:S(2)}, u32[]{:S(2)}) %collective-permute-start.1) | collective-permute-done | bytes 208928 | tf_op jit(solution)/shard_map/ppermute | solution.py:443
  41.9 1.1 %collective-permute-done = f32[24,1,2176]{2,1,0:T(1,128)S(1)} collective-permute-done((f32[24,1,2176]{2,1,0:T(1,128)S(1)}, f32[24,1,2176]{2,1,0:T(1,128)S(1)}, u32[]{:S(2)}, u32[]{:S(2)}) %collective-permute-start) | collective-permute-done | bytes 208928 | tf_op jit(solution)/shard_map/ppermute | solution.py:444
  43.0 5.4 %solve.1 = f32[512,128]{1,0:T(8,128)S(1)} custom-call(f32[2]{0:T(128)} %bounds_hbm.1, f32[1088,128]{1,0:T(8,128)S(1)} %bitcast.8, f32[408,128]{1,0:T(8,128)S(1)} %bitcast.14, f32[408,128]{1,0:T(8,128)S(1)} %bitcast.13, f32[408,128]{1,0:T(8,128)S(1)} %bitcast.12, f32[4,128,128]{2,1,0:T(8,128)S(1)} %get-tuple-element.13.own_x_ref, ...), custom_call_target="tpu_custom_call" | custom-call | tf_op jit(solution)/shard_map/solve/pallas_call | solution.py:387
  48.5 0.0 copy-start
  48.5 18.7 %all_to_all.11 = f32[64,8,128]{2,1,0:T(8,128)S(1)} all-to-all(f32[64,8,128]{2,1,0:T(8,128)S(1)} %bitcast.11), channel_id=1, replica_groups=mesh['region'=8,'blk'=64] {'blk'}, dimensions={0} | all-to-all | bytes 524288 | tf_op jit(solution)/shard_map/all_to_all | solution.py:448
  67.2 0.0 copy-done
  67.2 0.7 %add.1 = f32[2,256,128]{2,1,0:T(8,128)} custom-call(f32[2,256,128]{2,1,0:T(8,128)S(1)} %copy-done, f32[32,2,8,128]{3,2,1,0:T(8,128)S(1)} %bitcast.10), custom_call_target="tpu_custom_call" | custom-call | tf_op jit(solution)/shard_map/add/pallas_call | solution.py:449
Async XLA Ops:
  30.4 9.2 %collective-permute-start.2 = (f32[24,1,2176]{2,1,0:T(1,128)S(1)}, f32[24,1,2176]{2,1,0:T(1,128)S(1)}, u32[]{:S(2)}, u32[]{:S(2)}) collective-permute-start(f32[24,1,2176]{2,1,0:T(1,128)S(1)} %get-tuple-element.17), channel_id=1, source_target_pairs={{64,0},{66,2},{68,4},{70,6},{72,8},{74,10},{76,12},{78,14},{80,16}... | collective-permute-start | bytes 626696 | tf_op jit(solution)/shard_map/ppermute | solution.py:442
  31.1 10.8 %collective-permute-start.1 = (f32[24,1,2176]{2,1,0:T(1,128)S(1)}, f32[24,1,2176]{2,1,0:T(1,128)S(1)}, u32[]{:S(2)}, u32[]{:S(2)}) collective-permute-start(f32[24,1,2176]{2,1,0:T(1,128)S(1)} %get-tuple-element.18), channel_id=1, source_target_pairs={{65,1},{67,3},{69,5},{71,7},{73,9},{75,11},{77,13},{79,15},{81,17}... | collective-permute-start | bytes 626696 | tf_op jit(solution)/shard_map/ppermute | solution.py:443
  33.1 10.0 %collective-permute-start = (f32[24,1,2176]{2,1,0:T(1,128)S(1)}, f32[24,1,2176]{2,1,0:T(1,128)S(1)}, u32[]{:S(2)}, u32[]{:S(2)}) collective-permute-start(f32[24,1,2176]{2,1,0:T(1,128)S(1)} %get-tuple-element.19), channel_id=1, source_target_pairs={{1,65},{3,67},{5,69},{7,71},{9,73},{11,75},{13,77},{15,79},{17,81}... | collective-permute-start | bytes 626696 | tf_op jit(solution)/shard_map/ppermute | solution.py:444
  48.5 18.7 %copy-start = (f32[2,256,128]{2,1,0:T(8,128)S(1)}, f32[2,256,128]{2,1,0:T(8,128)}, u32[]{:S(2)}) copy-start(f32[2,256,128]{2,1,0:T(8,128)} %ens_ref.1) | copy-start | bytes 786436

commit v9 on v8

--- a/solution.py
+++ b/solution.py
@@ -28,8 +28,8 @@
     pred_ref, ridge_ref, ens_ref, obs_ref, var_ref, sems,
 ):
     pairs = [
-        (ens_hbm, ens_ref), (var_hbm, var_ref), (pred_hbm, pred_ref), (ridge_hbm, ridge_ref),
-        (obs_hbm, obs_ref),
+        (ens_hbm.at[0], ens_ref.at[0]), (var_hbm, var_ref), (pred_hbm, pred_ref), (ridge_hbm, ridge_ref),
+        (ens_hbm.at[1], ens_ref.at[1]), (obs_hbm, obs_ref),
     ]
     copies = [pltpu.make_async_copy(a, b, sems.at[i]) for i, (a, b) in enumerate(pairs)]
     for copy in copies:
@@ -59,6 +59,8 @@
         for k in range(slots):
             meta = jnp.where(spot == META * b + k, pred_ref[b, k].astype(jnp.float32), meta)
         meta = jnp.where(spot == META * b + slots, ridge_ref[b], meta)
+        if b == 1:
+            copies[4].wait()
         ens = ens_ref[b]
         anomaly = (ens - jnp.mean(ens, axis=1, keepdims=True)) * (1.0 / (members - 1) ** 0.5)
         folded = anomaly + anomaly[:, last:] * (1.0 / (members**0.5 - 1.0))
@@ -67,7 +69,7 @@
     deal(blocks, 0)
     for p in range(2 * groups):
         out_ref[p * CHUNK + FIRST - 1 : p * CHUNK + FIRST, :] = meta
-    copies[4].wait()
+    copies[5].wait()
     deal([obs_ref[b] - ens_ref[b] for b in range(local_blocks)], FIRST)
 
 
@@ -354,7 +356,7 @@
             pltpu.VMEM(ensemble.shape, jnp.float32),
             pltpu.VMEM(observed.shape, jnp.float32),
             pltpu.VMEM(obs_var.shape, jnp.float32),
-            pltpu.SemaphoreType.DMA((5,)),
+            pltpu.SemaphoreType.DMA((6,)),
         ],
         compiler_params=PARAMS,
         name="pack",

time: 68.2 us -> 68.4 us (level)
  the two profiles are of different devices: /device:TPU:193 before, /device:TPU:257 now
where the time goes in v9:
time: 68.4 us; the launch traced here: 68.2 us
  blocking collectives  47.7 us (70%)
  Pallas kernels  9.03 us (13%)
  starting transfers between devices  5.96 us (9%)
  waiting for transfers between devices  5.36 us (8%)
    all_to_all x1, blocking collectives, on_device(): lax.all_to_all(packed.reshape(peers, 1, CHUNK * members), 'blk', 0, 0, ti...  29 us
    all_to_all x1, blocking collectives, on_device(): increment = lax.all_to_all(increment, 'blk', 0, 0, tiled=True)  18.7 us
    pallas_call x1, Pallas kernels, solve(): pl.pallas_call(solve_kernel, out_shape=jax.ShapeDtypeStruct((own.shape[0]...  5.43 us
    ppermute x1, starting transfers between devices, on_device(): third = lax.ppermute(own[peers - edge:], AXES, pairs(1, 1))  3.36 us
    ppermute x1, waiting for transfers between devices, on_device(): third = lax.ppermute(own[peers - edge:], AXES, pairs(1, 1))  3.14 us
    ppermute x1, waiting for transfers between devices, on_device(): second = lax.ppermute(middle, AXES, pairs(1, -1) + pairs(0, 1))  2.22 us
    ppermute x1, starting transfers between devices, on_device(): second = lax.ppermute(middle, AXES, pairs(1, -1) + pairs(0, 1))  1.92 us
    pallas_call x1, Pallas kernels, pack(): pl.pallas_call(pack_kernel, out_shape=pltpu.VMEM((peers * CHUNK, members)...  1.54 us
  transfers between devices with their start and end apart: 3, of which 2 were waited for; matrix products, arithmetic and copies ran while one was open for 0% of the time, Pallas kernels for 2%

profile of v9, /device:TPU:257, one launch (start us, length us, event | category | flops | bytes accessed | tf_op | source)
XLA Modules:
  0.0 68.2 jit_solution(2456217447892611017)
XLA Ops:
  0.0 1.5 %pack.1 = f32[1088,128]{1,0:T(8,128)S(1)} custom-call(s32[2,12]{1,0:T(2,128)} %pred_hbm.1, f32[2]{0:T(128)} %ridge_hbm.1, f32[2,256,128]{2,1,0:T(8,128)} %ens_ref.1, f32[2,256,128]{2,1,0:T(8,128)} %obs_hbm, f32[2,256]{1,0:T(2,128)} %var_hbm.1), custom_call_target="tpu_custom_call" | custom-call | tf_op jit(solution)/shard_map/pack/pallas_call | solution.py:348
  1.5 29.0 %all_to_all.10 = f32[64,1,2176]{2,1,0:T(1,128)S(1)} all-to-all(f32[64,1,2176]{2,1,0:T(1,128)S(1)} %bitcast.9), channel_id=1, replica_groups=mesh['region'=8,'blk'=64] {'blk'}, dimensions={0} | all-to-all | bytes 1114112 | tf_op jit(solution)/shard_map/all_to_all | solution.py:430
  30.5 0.1 fusion
  30.6 0.7 collective-permute-start.2
  31.3 1.9 %collective-permute-start.1 = (f32[24,1,2176]{2,1,0:T(1,128)S(1)}, f32[24,1,2176]{2,1,0:T(1,128)S(1)}, u32[]{:S(2)}, u32[]{:S(2)}) collective-permute-start(f32[24,1,2176]{2,1,0:T(1,128)S(1)} %get-tuple-element.18), channel_id=1, source_target_pairs={{65,1},{67,3},{69,5},{71,7},{73,9},{75,11},{77,13},{79,15},{81,17}... | collective-permute-start | bytes 626696 | tf_op jit(solution)/shard_map/ppermute | solution.py:445
  33.2 3.4 %collective-permute-start = (f32[24,1,2176]{2,1,0:T(1,128)S(1)}, f32[24,1,2176]{2,1,0:T(1,128)S(1)}, u32[]{:S(2)}, u32[]{:S(2)}) collective-permute-start(f32[24,1,2176]{2,1,0:T(1,128)S(1)} %get-tuple-element.19), channel_id=1, source_target_pairs={{1,65},{3,67},{5,69},{7,71},{9,73},{11,75},{13,77},{15,79},{17,81}... | collective-permute-start | bytes 626696 | tf_op jit(solution)/shard_map/ppermute | solution.py:446
  36.6 1.3 %local.1 = (f32[4,128,128]{2,1,0:T(8,128)S(1)}, f32[4,128,128]{2,1,0:T(8,128)S(1)}, f32[8,128]{1,0:T(8,128)S(1)}, f32[17,4,128]{2,1,0:T(4,128)S(1)}) custom-call(f32[1088,128]{1,0:T(8,128)S(1)} %bitcast.7), custom_call_target="tpu_custom_call" | custom-call | tf_op jit(solution)/shard_map/local/pallas_call | solution.py:369
  37.9 0.0 collective-permute-done.2
  37.9 2.2 %collective-permute-done.1 = f32[24,1,2176]{2,1,0:T(1,128)S(1)} collective-permute-done((f32[24,1,2176]{2,1,0:T(1,128)S(1)}, f32[24,1,2176]{2,1,0:T(1,128)S(1)}, u32[]{:S(2)}, u32[]{:S(2)}) %collective-permute-start.1) | collective-permute-done | bytes 208928 | tf_op jit(solution)/shard_map/ppermute | solution.py:445
  40.1 3.1 %collective-permute-done = f32[24,1,2176]{2,1,0:T(1,128)S(1)} collective-permute-done((f32[24,1,2176]{2,1,0:T(1,128)S(1)}, f32[24,1,2176]{2,1,0:T(1,128)S(1)}, u32[]{:S(2)}, u32[]{:S(2)}) %collective-permute-start) | collective-permute-done | bytes 208928 | tf_op jit(solution)/shard_map/ppermute | solution.py:446
  43.3 5.4 %solve.1 = f32[512,128]{1,0:T(8,128)S(1)} custom-call(f32[2]{0:T(128)} %bounds_hbm.1, f32[1088,128]{1,0:T(8,128)S(1)} %bitcast.8, f32[408,128]{1,0:T(8,128)S(1)} %bitcast.14, f32[408,128]{1,0:T(8,128)S(1)} %bitcast.13, f32[408,128]{1,0:T(8,128)S(1)} %bitcast.12, f32[4,128,128]{2,1,0:T(8,128)S(1)} %get-tuple-element.13.own_x_ref, ...), custom_call_target="tpu_custom_call" | custom-call | tf_op jit(solution)/shard_map/solve/pallas_call | solution.py:389
  48.7 0.0 copy-start
  48.7 18.7 %all_to_all.11 = f32[64,8,128]{2,1,0:T(8,128)S(1)} all-to-all(f32[64,8,128]{2,1,0:T(8,128)S(1)} %bitcast.11), channel_id=1, replica_groups=mesh['region'=8,'blk'=64] {'blk'}, dimensions={0} | all-to-all | bytes 524288 | tf_op jit(solution)/shard_map/all_to_all | solution.py:450
  67.4 0.0 copy-done
  67.4 0.7 %add.1 = f32[2,256,128]{2,1,0:T(8,128)} custom-call(f32[2,256,128]{2,1,0:T(8,128)S(1)} %copy-done, f32[32,2,8,128]{3,2,1,0:T(8,128)S(1)} %bitcast.10), custom_call_target="tpu_custom_call" | custom-call | tf_op jit(solution)/shard_map/add/pallas_call | solution.py:451
Async XLA Ops:
  30.6 7.3 %collective-permute-start.2 = (f32[24,1,2176]{2,1,0:T(1,128)S(1)}, f32[24,1,2176]{2,1,0:T(1,128)S(1)}, u32[]{:S(2)}, u32[]{:S(2)}) collective-permute-start(f32[24,1,2176]{2,1,0:T(1,128)S(1)} %get-tuple-element.17), channel_id=1, source_target_pairs={{64,0},{66,2},{68,4},{70,6},{72,8},{74,10},{76,12},{78,14},{80,16}... | collective-permute-start | bytes 626696 | tf_op jit(solution)/shard_map/ppermute | solution.py:444
  31.3 8.9 %collective-permute-start.1 = (f32[24,1,2176]{2,1,0:T(1,128)S(1)}, f32[24,1,2176]{2,1,0:T(1,128)S(1)}, u32[]{:S(2)}, u32[]{:S(2)}) collective-permute-start(f32[24,1,2176]{2,1,0:T(1,128)S(1)} %get-tuple-element.18), channel_id=1, source_target_pairs={{65,1},{67,3},{69,5},{71,7},{73,9},{75,11},{77,13},{79,15},{81,17}... | collective-permute-start | bytes 626696 | tf_op jit(solution)/shard_map/ppermute | solution.py:445
  33.2 10.1 %collective-permute-start = (f32[24,1,2176]{2,1,0:T(1,128)S(1)}, f32[24,1,2176]{2,1,0:T(1,128)S(1)}, u32[]{:S(2)}, u32[]{:S(2)}) collective-permute-start(f32[24,1,2176]{2,1,0:T(1,128)S(1)} %get-tuple-element.19), channel_id=1, source_target_pairs={{1,65},{3,67},{5,69},{7,71},{9,73},{11,75},{13,77},{15,79},{17,81}... | collective-permute-start | bytes 626696 | tf_op jit(solution)/shard_map/ppermute | solution.py:446
  48.7 18.7 %copy-start = (f32[2,256,128]{2,1,0:T(8,128)S(1)}, f32[2,256,128]{2,1,0:T(8,128)}, u32[]{:S(2)}) copy-start(f32[2,256,128]{2,1,0:T(8,128)} %ens_ref.1) | copy-start | bytes 786436
